TPU v7x, 512 devices: a whole 4x4x16 slice. The times are simulated.
512 devices in a mesh: pulse: 4 (over z_lo), range: 4 (over y), tile: 32 (over z_hi, x, core).
Axes of the slice: x: 4, y: 4, z: 16 (z_hi: 4, z_lo: 4; z = z_hi * 4 + z_lo), core: 2. Of those that a mesh axis runs over, the one named last changes fastest.
Arguments:
- echo: bfloat16 [2, 1024, 32768], P(None, ('pulse', 'tile'), 'range'), may hold values from -6 to 6
- replica: bfloat16 [2, 4096], replicated, may hold values from -0.09375 to 0.09375
- interp: bfloat16 [32, 256, 128], P('range'), may hold values from -0.375 to 0.375
- band_start: int32 [1024, 32, 4], P(('pulse', 'tile'), None, 'range'), may hold values from 0 to 7040, as said below
- visible: int32 [1024, 32], P(('pulse', 'tile')), may hold values 0 or 1
- doppler: int32 [1024], P(('pulse', 'tile')), may hold values from 0 to 8191
- range_step: int32 [1024], P(('pulse', 'tile')), may hold values from 0 to 4095
Outputs:
- image: float32 [2, 8192, 4096], P(None, ('tile', 'pulse'), 'range')
Inputs may be any that keep to these rules, and one draw needn't show every extreme that they name: band_start is counted within the 8192 bins of range block b and is a multiple of 128; the values 0 and 7040 both occur.
All inputs are finite; a program needn't handle non-finite values. No bound on the sum of `visible` on one device may be relied on, other than what follows from the above.
Results may differ from a plain program's by a relative error of at most 0.0047.
Values may be sent and summed in bfloat16 or wider, within the bound.
No kernel may reach another device: no remote copies, remote signals or barrier semaphores. Data moves between devices by JAX's collectives and lax.ppermute only.
A program may use at most 64 MiB of HBM per device.

v0:
```python
import math

import jax
import jax.numpy as jnp
from jax import lax
from jax.sharding import PartitionSpec as P

AZ_DEV = 64


def padded_2(cells, sides, width):
    for axis, dim in sides:
        count = lax.axis_size(axis)
        ends = count - 1
        head = lax.slice_in_dim(cells, 0, width, axis=dim)
        tail = lax.slice_in_dim(cells, cells.shape[dim] - width, cells.shape[dim], axis=dim)
        cells = jnp.concatenate(
            [
                lax.ppermute(tail, axis, [(i, (i + 1) % count) for i in range(ends)]),
                cells,
                lax.ppermute(head, axis, [((i + 1) % count, i) for i in range(ends)]),
            ],
            axis=dim,
        )
    return cells


def toeplitz_block(padded, offset, block_width):
    segment = lax.dynamic_slice_in_dim(padded, offset, 2 * block_width + 1)
    repeated = jnp.tile(segment, block_width)[: 2 * block_width * block_width]
    skewed = repeated.reshape(block_width, 2 * block_width)
    return skewed[:, block_width:].T


def chirp_matrix(padded_real, padded_imag, offset, block_width):
    toep_real = toeplitz_block(padded_real, offset, block_width)
    toep_imag = toeplitz_block(padded_imag, offset, block_width)
    upper_rows = jnp.concatenate([toep_real, -toep_imag], axis=1)
    lower_rows = jnp.concatenate([toep_imag, toep_real], axis=1)
    return jnp.concatenate([upper_rows, lower_rows], axis=0)


def compress(extended, replica, block_width):
    chirp_len = replica.shape[1]
    pulses = extended.shape[1]
    total_blocks = extended.shape[2] // block_width
    out_blocks = total_blocks - chirp_len // block_width
    arranged = extended.reshape(2, pulses, total_blocks, block_width).transpose(1, 2, 0, 3)
    margin = jnp.zeros((2, block_width), replica.dtype)
    padded = jnp.concatenate([margin, replica, margin, margin[:, :1]], axis=1)

    def add_turn(turn_index, running):
        offset = (turn_index * block_width).astype(jnp.int32)
        matrix = chirp_matrix(padded[0], padded[1], offset, block_width)
        window = lax.dynamic_slice_in_dim(arranged, turn_index.astype(jnp.int32), out_blocks, 1)
        window = window.reshape(pulses * out_blocks, 2 * block_width)
        return running + jnp.dot(window, matrix, preferred_element_type=jnp.float32)

    start_total = jnp.zeros((pulses * out_blocks, 2 * block_width), jnp.float32)
    running = lax.fori_loop(0, chirp_len // block_width + 1, add_turn, start_total)
    shaped = running.reshape(pulses, out_blocks, 2, block_width).transpose(0, 2, 1, 3)
    return shaped.reshape(pulses, 2, out_blocks * block_width).astype(jnp.bfloat16)


def select_bands(signals, first_bins, band_len, line_block):
    pulses = signals.shape[0]
    block_total = signals.shape[2] // line_block
    band_blocks = band_len // line_block
    pieces = signals.reshape(pulses, 2, block_total, line_block)
    wanted = first_bins[:, None] // line_block + jnp.arange(band_blocks, dtype=jnp.int32)[None, :]
    chooser = (
        wanted[:, :, None] == jnp.arange(block_total, dtype=jnp.int32)[None, None, :]
    ).astype(jnp.bfloat16)
    picked = jnp.einsum("pjk,pckl->pcjl", chooser, pieces, preferred_element_type=jnp.float32)
    return picked.astype(jnp.bfloat16).reshape(pulses, 2, band_len)


def steer_lines(band_rows, interp_block, range_steps, first_line, range_total):
    pulses = band_rows.shape[0]
    block_count = interp_block.shape[0]
    line_block = interp_block.shape[2]
    pieces = band_rows.reshape(pulses, 2, block_count + 1, line_block)
    windows = jnp.concatenate([pieces[:, :, :-1], pieces[:, :, 1:]], axis=3)
    line_values = jnp.einsum(
        "pcjb,jbl->pcjl", windows, interp_block, preferred_element_type=jnp.float32
    )
    line_values = line_values.reshape(pulses, 2, block_count * line_block)
    line_number = first_line + jnp.arange(block_count * line_block, dtype=jnp.int32)
    phase_turns = range_steps[:, None] * line_number[None, :] % range_total
    phase_angle = phase_turns.astype(jnp.float32) * (2.0 * math.pi / range_total)
    cosine = jnp.cos(phase_angle)
    sine_part = jnp.sin(phase_angle)
    steered_real = line_values[:, 0] * cosine - line_values[:, 1] * sine_part
    steered_imag = line_values[:, 0] * sine_part + line_values[:, 1] * cosine
    return jnp.stack([steered_real, steered_imag], axis=1).astype(jnp.bfloat16)


def azimuth_factor(doppler_bins, visible_flags, line_number, azimuth_total, norm_scale):
    phase_turns = line_number[:, None] * doppler_bins[None, :] % azimuth_total
    phase_angle = phase_turns.astype(jnp.float32) * (2.0 * math.pi / azimuth_total)
    weight = visible_flags.astype(jnp.float32)[None, :] * norm_scale
    factor_real = (jnp.cos(phase_angle) * weight).astype(jnp.bfloat16)
    factor_imag = (jnp.sin(phase_angle) * weight).astype(jnp.bfloat16)
    return (factor_real, factor_imag)


def add_pulses(factor_real, factor_imag, steered):
    left_side = jnp.concatenate([factor_real, factor_imag], axis=1)
    steer_real = steered[:, 0]
    steer_imag = steered[:, 1]
    top_rows = jnp.concatenate([steer_real, steer_imag], axis=1)
    bottom_rows = jnp.concatenate([-steer_imag, steer_real], axis=1)
    right_side = jnp.concatenate([top_rows, bottom_rows], axis=0)
    return jnp.dot(left_side, right_side, preferred_element_type=jnp.float32)


def local(echo, replica, interp, band_start, visible, doppler, range_step):
    chirp_len = replica.shape[1]
    half_chirp = chirp_len // 2
    block_width = min(256, half_chirp)
    pulses_dev = echo.shape[1]
    line_block = interp.shape[2]
    lines_dev = interp.shape[0] * line_block
    band_len = lines_dev + line_block
    tile_count = lax.axis_size("tile")
    pulse_count = lax.axis_size("pulse")
    range_total = lines_dev * lax.axis_size("range")
    azimuth_total = AZ_DEV * pulse_count * tile_count
    group_pulses = pulses_dev * tile_count
    norm_scale = (pulses_dev * pulse_count * tile_count) ** (-0.5)
    tile_number = lax.axis_index("tile")
    first_line = lax.axis_index("range") * lines_dev
    extended = padded_2(echo, (("range", 2),), half_chirp)
    compressed = compress(extended, replica, block_width)
    empty_index = jnp.zeros((group_pulses,), jnp.int32)
    first_row = jnp.int32(0)
    signals = lax.all_gather(compressed, "tile", axis=0, tiled=True)
    starts_in = lax.all_gather(band_start, "tile", axis=0, tiled=True)
    flags_in = lax.all_gather(visible, "tile", axis=0, tiled=True)
    doppler_in = lax.all_gather(doppler, "tile", axis=0, tiled=True)
    steps_in = lax.all_gather(range_step, "tile", axis=0, tiled=True)
    first_bins = lax.dynamic_index_in_dim(starts_in[:, :, 0], tile_number, 1, keepdims=False)
    flags_tile = lax.dynamic_index_in_dim(flags_in, tile_number, 1, keepdims=False)
    band_rows = select_bands(signals, first_bins, band_len, line_block)
    steered_in = steer_lines(band_rows, interp, steps_in, first_line, range_total)
    doppler_all = lax.dynamic_update_slice_in_dim(empty_index, doppler_in, first_row, 0)
    flags_all = lax.dynamic_update_slice_in_dim(empty_index, flags_tile, first_row, 0)
    tile_first = tile_number * (pulse_count * AZ_DEV)
    strip_lines = tile_first + jnp.arange(pulse_count * AZ_DEV, dtype=jnp.int32)
    factor_real, factor_imag = azimuth_factor(
        doppler_all, flags_all, strip_lines, azimuth_total, norm_scale
    )
    partial_image = add_pulses(factor_real, factor_imag, steered_in)
    image_rows = lax.psum_scatter(partial_image, "pulse", scatter_dimension=0, tiled=True)
    return image_rows.reshape(AZ_DEV, 2, lines_dev).transpose(1, 0, 2)


def solution(mesh):
    in_specs = (
        P(None, ("pulse", "tile"), "range"),
        P(),
        P("range", None, None),
        P(("pulse", "tile"), None, "range"),
        P(("pulse", "tile"), None),
        P(("pulse", "tile")),
        P(("pulse", "tile")),
    )
    out_specs = P(None, ("tile", "pulse"), "range")
    return jax.shard_map(local, mesh=mesh, in_specs=in_specs, out_specs=out_specs, check_vma=False)
```

profile of v0, /device:TPU:1, one launch (start us, length us, event | category | flops | bytes accessed | tf_op | source)
XLA Modules:
  0.0 323.4 jit_solution(15231582714423784350)
XLA Ops:
  6.5 0.9 fusion.47
  7.5 1.3 collective-permute-start.1
  8.8 4.7 %collective-permute-start = (bf16[2,8,2048]{2,1,0:T(8,128)(2,1)S(1)}, bf16[2,8,2048]{2,1,0:T(8,128)(2,1)S(1)}, u32[]{:S(2)}, u32[]{:S(2)}) collective-permute-start(bf16[2,8,2048]{2,1,0:T(8,128)(2,1)S(1)} %get-tuple-element.126), channel_id=1, source_target_pairs={{0,32},{32,64},{64,96},{1,33},{33,65},{65,97},{2,34},{34,66},{66,9... | collective-permute-start | bytes 196616 | tf_op jit(solution)/shard_map/ppermute | solution.py:19
  13.5 0.7 maximum_maximum_fusion
  14.8 1.0 pad_maximum_fusion.1
  15.8 45.2 %while.14 = (s32[]{:T(128)}, f32[256,512]{1,0:T(8,128)S(1)}, bf16[8,48,2,256]{3,1,0,2:T(8,128)(2,1)S(1)}, bf16[2,4609]{1,0:T(2,128)(2,1)S(1)}, s32[]{:T(128)}, /*index=5*/s32[]{:T(128)}, s32[]{:T(128)}, s32[]{:T(128)}) while((s32[]{:T(128)}, f32[256,512]{1,0:T(8,128)S(1)}, bf16[8,48,2,256]{3,1,0,2:T(8,128)(2,1)S(1)}, ...), condition=%wide.region_1.0_spmd.clone, body=%wide.region_0.0_spmd.clone.sunk | while | flops 136642560 | bytes 7779505 | solution.py:60
  17.2 0.6 tile.67
  24.4 0.6 tile.65
  27.0 0.6 tile.65
  29.7 0.6 tile.65
  30.5 0.6 tile.67
  32.3 0.6 tile.65
  33.2 0.6 tile.67
  35.9 0.6 tile.67
  38.5 0.6 tile.67
  45.6 0.6 tile.65
  48.3 0.6 tile.65
  61.3 0.8 convert_element_type.58
  62.1 1.2 dynamic-slice.7
  64.4 26.6 %all-reduce.2 = (s32[256]{0:T(256)S(1)}, s32[256]{0:T(256)S(1)}) all-reduce(s32[256]{0:T(256)S(1)} %dynamic-update-slice.1, s32[256]{0:T(256)S(1)} %dynamic-update-slice), channel_id=1, replica_groups=mesh['pulse'=4,'range'=4,'tile'=32] {'tile'}, use_global_device_ids=true, to_apply=%add.1 | all-reduce | flops 512 | bytes 4096
  91.0 53.7 %all_gather.16 = s32[256,32]{1,0:T(8,128)S(1)} all-gather(s32[8,32]{1,0:T(8,128)S(1)} %copy-done.1), channel_id=1, replica_groups=mesh['pulse'=4,'range'=4,'tile'=32] {'tile'}, dimensions={0}, use_global_device_ids=true | all-gather | bytes 33792 | tf_op jit(solution)/shard_map/all_gather | solution.py:139
  144.9 74.4 %all_gather.18 = s32[256,32,1]{1,2,0:T(1,128)S(1)} all-gather(s32[8,32,1]{1,2,0:T(1,128)S(1)} %copy-done.2), channel_id=1, replica_groups=mesh['pulse'=4,'range'=4,'tile'=32] {'tile'}, dimensions={0}, use_global_device_ids=true | all-gather | bytes 33792 | tf_op jit(solution)/shard_map/all_gather | solution.py:138
  219.3 5.0 %dynamic-slice_reduce_fusion.2 = s32[256]{0:T(256)S(1)} fusion(s32[256,32,1]{1,2,0:T(1,128)S(1)} %all_gather.18, s32[]{:T(128)S(6)} %select_n.53), kind=kLoop, calls=%fused_computation.65 | loop fusion | bytes 2052 | tf_op jit(solution)/shard_map/jit(dynamic_index_in_dim)/dynamic_slice | solution.py:142
  224.4 1.3 multiply_convert_fusion.1
  225.7 14.6 %reshape.259 = bf16[256,2,64,128]{3,2,1,0:T(8,128)(2,1)} reshape(bf16[256,2,8192]{2,1,0:T(2,128)(2,1)} %all-gather.2.cloned.1.call-done) | data formatting | bytes 16777216 | tf_op jit(solution)/shard_map/reshape | solution.py:69
  240.3 4.2 %convert_bitcast_fusion = bf16[256,2,9,128]{3,2,1,0:T(8,128)(2,1)S(1)} fusion(bf16[256,2,64,128]{3,2,1,0:T(8,128)(2,1)} %reshape.259, s32[256,9]{1,0:T(8,128)S(1)} %iota_add_fusion), kind=kOutput, calls=%fused_computation.26 | convolution fusion | flops 76234752 | bytes 9577472 | tf_op jit(solution)/shard_map/pjk,pckl->pcjl/dot_general | solution.py:74
  245.2 1.3 fusion.24
  246.7 5.1 %fusion.31 = bf16[256,1024]{0,1:T(8,128)(2,1)S(1)} fusion(f32[256,2,1024]{0,2,1:T(8,128)S(1)} %bitcast.71, s32[1024]{0:T(1024)S(1)} %iota_add_fusion.1, s32[256]{0:T(256)S(1)} %get-tuple-element.116), kind=kLoop, calls=%fused_computation.42 | loop fusion | flops 4718592 | bytes 2626560 | tf_op jit(solution)/shard_map/squeeze | solution.py:109
  251.7 5.1 %fusion.43 = (bf16[256,1024]{0,1:T(8,128)(2,1)S(1)}, bf16[256,1024]{0,1:T(8,128)(2,1)S(1)}) fusion(f32[256,2,1024]{0,2,1:T(8,128)S(1)} %bitcast.72, s32[1024]{0:T(1024)S(1)} %iota_add_fusion.1, s32[256]{0:T(256)S(1)} %get-tuple-element.116), kind=kLoop, calls=%fused_computation.75 | loop fusion | flops 5505024 | bytes 3150848 | tf_op jit(solution)/shard_map/neg | solution.py:112
  256.8 2.1 fusion.9
  258.9 55.8 %reduce-scatter.2.cloned.1.call-done = f32[64,2048]{1,0:T(8,128)} async-done(((f32[256,2048]{1,0:T(8,128)}), f32[64,2048]{1,0:T(8,128)}) %reduce-scatter.2.cloned.1.call-update) | async-done | bytes 524304 | tf_op jit(solution)/shard_map/reduce_scatter | solution.py:154
  314.7 1.9 copy.49
  (314 shorter events, 38.8 us)
Async XLA Ops:
  6.5 238.6 %copy-start = (bf16[8,256,128]{2,1,0:T(8,128)(2,1)S(1)}, bf16[8,256,128]{2,1,0:T(8,128)(2,1)}, u32[]{:S(2)}) copy-start(bf16[8,256,128]{2,1,0:T(8,128)(2,1)} %param.11) | copy-start | bytes 1572868
  6.5 219.2 %all-gather.2.cloned.1.call-start = ((), (), s32[]{:S(2)}) async-start(), calls=%async_computation.1 | async-start | bytes 8650752 | tf_op jit(solution)/shard_map/all_gather | solution.py:137
  7.5 6.8 %collective-permute-start.1 = (bf16[2,8,2048]{2,1,0:T(8,128)(2,1)S(1)}, bf16[2,8,2048]{2,1,0:T(8,128)(2,1)S(1)}, u32[]{:S(2)}, u32[]{:S(2)}) collective-permute-start(bf16[2,8,2048]{2,1,0:T(8,128)(2,1)S(1)} %get-tuple-element.127), channel_id=1, source_target_pairs={{32,0},{64,32},{96,64},{33,1},{65,33},{97,65},{34,2},{66,34},{98,6... | collective-permute-start | bytes 196616 | tf_op jit(solution)/shard_map/ppermute | solution.py:21
  8.8 6.0 %collective-permute-start = (bf16[2,8,2048]{2,1,0:T(8,128)(2,1)S(1)}, bf16[2,8,2048]{2,1,0:T(8,128)(2,1)S(1)}, u32[]{:S(2)}, u32[]{:S(2)}) collective-permute-start(bf16[2,8,2048]{2,1,0:T(8,128)(2,1)S(1)} %get-tuple-element.126), channel_id=1, source_target_pairs={{0,32},{32,64},{64,96},{1,33},{33,65},{65,97},{2,34},{34,66},{66,9... | collective-permute-start | bytes 196616 | tf_op jit(solution)/shard_map/ppermute | solution.py:19
  61.1 2.9 copy-start.3
  61.1 3.1 copy-start.4
  61.1 29.9 %copy-start.1 = (s32[8,32]{1,0:T(8,128)S(1)}, s32[8,32]{1,0:T(8,128)}, u32[]{:S(2)}) copy-start(s32[8,32]{1,0:T(8,128)} %param.13) | copy-start | bytes 3076
  61.1 83.8 %copy-start.2 = (s32[8,32,1]{1,2,0:T(1,128)S(1)}, s32[8,32,1]{1,2,0:T(1,128)}, u32[]{:S(2)}) copy-start(s32[8,32,1]{1,2,0:T(1,128)} %param.12) | copy-start | bytes 3076
  62.1 252.6 %reduce-scatter.2.cloned.1.call-start = ((), (), s32[]{:S(2)}) async-start(), calls=%async_computation.2 | async-start | bytes 2621440 | tf_op jit(solution)/shard_map/reduce_scatter | solution.py:154
Sparse Core Ops, SparseCore 0:
  62.2 145.3 all-gather.1
  259.0 55.6 reduce-scatter.1
where the time goes:
time: 324 us; the launch traced here: 323 us
  blocking collectives  155 us (48%)
  local copies, waits for them, and re-layouts  61.7 us (19%)
  waiting for transfers between devices  56.3 us (17%)
  matrix products  14.5 us (4%)
  between operations  14.2 us (4%)
  other arithmetic  13.9 us (4%)
  starting transfers between devices  6 us (2%)
    all_gather x1, blocking collectives, local(): starts_in = lax.all_gather(band_start, 'tile', axis=0, tiled=True)  74.4 us
    reduce_scatter x1, waiting for transfers between devices, local(): lax.psum_scatter(partial_image, 'pulse', scatter_dimension=0, tiled=True)  55.8 us
    all_gather x1, blocking collectives, local(): flags_in = lax.all_gather(visible, 'tile', axis=0, tiled=True)  53.7 us
    unnamed x1, blocking collectives  26.6 us
    another operation x68, local copies, waits for them, and re-layouts, toeplitz_block(): repeated = jnp.tile(segment, block_width)[:2 * block_width * block_width]  21.6 us
    reshape x1, local copies, waits for them, and re-layouts, select_bands(): pieces = signals.reshape(pulses, 2, block_total, line_block)  14.6 us
    dot_general x17, matrix products, add_turn(): return running + jnp.dot(window, matrix, preferred_element_type=jnp.float32)  6.84 us
  transfers between devices with their start and end apart: 4, of which 2 were waited for; matrix products, arithmetic and copies ran while one was open for 3% of the time, Pallas kernels for 0%

commit v1 on v0

v1 whole, which is shorter than its diff:
```python
import math

import jax
import jax.numpy as jnp
from jax import lax
from jax.experimental import pallas as pl
from jax.experimental.pallas import tpu as pltpu
from jax.sharding import PartitionSpec as P

AZ_DEV = 64
LANES = 128
VMEM_LIMIT = 48 * 1024 * 1024


def skew_kernel(flip_ref, real_ref, imag_ref, minus_ref):
    count = real_ref.shape[1] // LANES
    for part, target in ((0, real_ref), (1, imag_ref)):
        for block in range(count):
            window = flip_ref[part : part + 1, block * LANES : (block + 2) * LANES]
            wide = jnp.broadcast_to(window, (LANES, 2 * LANES))
            rolled = pltpu.roll(wide, 1, 1, stride=1, stride_axis=0)[:, LANES:]
            place = slice(block * LANES, (block + 1) * LANES)
            target[:, place] = rolled.astype(jnp.bfloat16)
            if part == 1:
                minus_ref[:, place] = (-rolled).astype(jnp.bfloat16)


def skew_matrices(replica):
    taps = replica.shape[1]
    width = taps + LANES
    flipped = jnp.pad(jnp.flip(replica.astype(jnp.float32), 1), ((0, 0), (LANES, LANES)))
    shape = jax.ShapeDtypeStruct((LANES, width), jnp.bfloat16)
    return pl.pallas_call(
        skew_kernel,
        out_shape=(shape, shape, shape),
        name="skew_matrices",
        compiler_params=pltpu.CompilerParams(vmem_limit_bytes=VMEM_LIMIT),
        cost_estimate=pl.CostEstimate(flops=4000000, bytes_accessed=4 * 1024 * 1024, transcendentals=0),
    )(flipped)


def steer_kernel(
    left_ref, own_ref, right_ref, real_ref, imag_ref, minus_ref, interp_ref, target_ref,
    cos_ref, sin_ref, out_ref, even_ref, odd_ref, total_ref, band_ref,
):
    pulses = own_ref.shape[1]
    left_blocks = left_ref.shape[2] // LANES
    own_blocks = own_ref.shape[2] // LANES
    turns = real_ref.shape[1] // LANES
    blocks = 2 * left_blocks + own_blocks
    line_blocks = interp_ref.shape[0]
    rows = target_ref.shape[0]
    tiles = rows // pulses

    def cells(block):
        if block < left_blocks:
            ref, at = left_ref, block
        elif block < left_blocks + own_blocks:
            ref, at = own_ref, block - left_blocks
        else:
            ref, at = right_ref, block - left_blocks - own_blocks
        place = slice(at * LANES, (at + 1) * LANES)
        return jnp.concatenate(
            [ref[0, :, place].astype(jnp.float32), ref[1, :, place].astype(jnp.float32)], axis=1
        )

    for pair in range(blocks // 2):
        both = jnp.concatenate([cells(2 * pair), cells(2 * pair + 1)], axis=0)
        even_ref[pair] = both.astype(jnp.bfloat16)
        if 2 * pair + 2 < blocks:
            both = jnp.concatenate([cells(2 * pair + 1), cells(2 * pair + 2)], axis=0)
            odd_ref[pair] = both.astype(jnp.bfloat16)

    for turn in range(turns):
        source = even_ref if turn % 2 == 0 else odd_ref
        first = turn // 2
        window = source[first : first + own_blocks // 2].reshape(own_blocks * pulses, 2 * LANES)
        place = slice((turns - 1 - turn) * LANES, (turns - turn) * LANES)
        upper = jnp.concatenate([real_ref[:, place], minus_ref[:, place]], axis=1)
        lower = jnp.concatenate([imag_ref[:, place], real_ref[:, place]], axis=1)
        matrix = jnp.concatenate([upper, lower], axis=0)
        product = jnp.dot(window, matrix, preferred_element_type=jnp.float32)
        if turn == 0:
            total_ref[...] = product
        else:
            total_ref[...] += product

    compressed = total_ref[...].astype(jnp.bfloat16)
    column = lax.broadcasted_iota(jnp.int32, (rows, own_blocks * pulses), 1)
    for piece in range(line_blocks + 1):
        chooser = jnp.where(column == target_ref[...] + piece * pulses, 1.0, 0.0).astype(jnp.bfloat16)
        picked = jnp.dot(chooser, compressed, preferred_element_type=jnp.float32)
        band_ref[piece] = picked.astype(jnp.bfloat16)

    for line in range(line_blocks):
        values = []
        for part in range(2):
            half = slice(part * LANES, (part + 1) * LANES)
            pair = jnp.concatenate([band_ref[line, :, half], band_ref[line + 1, :, half]], axis=1)
            value = jnp.dot(pair, interp_ref[line], preferred_element_type=jnp.float32)
            values.append(value.reshape(tiles, pulses, LANES))
        place = slice(line * LANES, (line + 1) * LANES)
        cosine = cos_ref[:, place][None]
        sine = sin_ref[:, place][None]
        steer_real = values[0] * cosine - values[1] * sine
        steer_imag = values[0] * sine + values[1] * cosine
        steered = jnp.concatenate([steer_real, steer_imag], axis=1)
        out_ref[:, :, place] = steered.astype(jnp.bfloat16)


def steered_values(left, echo, right, skewed, interp, targets, cosine, sine):
    pulses = echo.shape[1]
    own_blocks = echo.shape[2] // LANES
    blocks = own_blocks + 2 * (left.shape[2] // LANES)
    rows = targets.shape[0]
    line_blocks = interp.shape[0]
    return pl.pallas_call(
        steer_kernel,
        out_shape=jax.ShapeDtypeStruct((rows // pulses, 2 * pulses, line_blocks * LANES), jnp.bfloat16),
        scratch_shapes=[
            pltpu.VMEM((blocks // 2, 2 * pulses, 2 * LANES), jnp.bfloat16),
            pltpu.VMEM((blocks // 2, 2 * pulses, 2 * LANES), jnp.bfloat16),
            pltpu.VMEM((own_blocks * pulses, 2 * LANES), jnp.float32),
            pltpu.VMEM((line_blocks + 1, rows, 2 * LANES), jnp.bfloat16),
        ],
        name="steered_values",
        compiler_params=pltpu.CompilerParams(vmem_limit_bytes=VMEM_LIMIT),
        cost_estimate=pl.CostEstimate(flops=4000000000, bytes_accessed=6 * 1024 * 1024, transcendentals=0),
    )(left, echo, right, *skewed, interp, targets, cosine, sine)


def local(echo, replica, interp, band_start, visible, doppler, range_step):
    half_chirp = replica.shape[1] // 2
    pulses_dev = echo.shape[1]
    line_block = interp.shape[2]
    lines_dev = interp.shape[0] * line_block
    tile_count = lax.axis_size("tile")
    pulse_count = lax.axis_size("pulse")
    range_count = lax.axis_size("range")
    range_total = lines_dev * range_count
    azimuth_total = AZ_DEV * pulse_count * tile_count
    norm_scale = (pulses_dev * pulse_count * tile_count) ** (-0.5)
    tile_number = lax.axis_index("tile")
    first_line = lax.axis_index("range") * lines_dev

    up = [(i, i + 1) for i in range(range_count - 1)]
    down = [(i + 1, i) for i in range(range_count - 1)]
    left = lax.ppermute(echo[:, :, -half_chirp:], "range", up)
    right = lax.ppermute(echo[:, :, :half_chirp], "range", down)
    skewed = skew_matrices(replica)

    doppler_rows = lax.optimization_barrier(jnp.broadcast_to(doppler[:, None], (pulses_dev, LANES)))
    doppler_rows = lax.all_gather(doppler_rows, "tile", axis=0, tiled=True)
    doppler_rows = lax.optimization_barrier(doppler_rows)
    doppler_in = doppler_rows[:, 0].reshape(tile_count, 1, pulses_dev)

    line_number = first_line + jnp.arange(lines_dev, dtype=jnp.int32)
    phase_turns = range_step[:, None] * line_number[None, :] % range_total
    phase_angle = phase_turns.astype(jnp.float32) * (2.0 * math.pi / range_total)
    cosine = jnp.cos(phase_angle)
    sine = jnp.sin(phase_angle)

    pulse_index = jnp.arange(pulses_dev, dtype=jnp.int32)[:, None]
    targets = band_start[:, :, 0] // LANES * pulses_dev + pulse_index
    targets = jnp.where(visible != 0, targets, -(1 << 20)).T.reshape(tile_count * pulses_dev, 1)

    steered = steered_values(left, echo, right, skewed, interp, targets, cosine, sine)
    arrived = lax.all_to_all(steered, "tile", 0, 0, tiled=True)
    columns = tile_count * 2 * pulses_dev
    arrived = arrived.reshape(columns, lines_dev)

    quarter = azimuth_total // 4
    shape = (pulse_count, 2, AZ_DEV, tile_count, 2, pulses_dev)
    axes = [lax.broadcasted_iota(jnp.int32, shape[:3], axis) for axis in range(3)]
    lines = tile_number * (pulse_count * AZ_DEV) + axes[0] * AZ_DEV + axes[2]
    lines = lines.reshape(-1, 1)
    out_part = axes[1].reshape(-1, 1)
    in_part = jnp.broadcast_to(
        jnp.arange(2, dtype=jnp.int32)[None, :, None], (tile_count, 2, pulses_dev)
    ).reshape(1, -1)
    bins = jnp.broadcast_to(doppler_in, (tile_count, 2, pulses_dev)).reshape(1, -1)
    azimuth_turns = (lines * bins + (in_part - out_part) * quarter) % azimuth_total
    azimuth_angle = azimuth_turns.astype(jnp.float32) * (2.0 * math.pi / azimuth_total)
    factor = (jnp.cos(azimuth_angle) * norm_scale).astype(jnp.bfloat16)
    factor = lax.optimization_barrier(factor)

    partial_image = jnp.dot(factor, arrived, preferred_element_type=jnp.float32).astype(jnp.bfloat16)
    image_rows = lax.psum_scatter(partial_image, "pulse", scatter_dimension=0, tiled=True)
    return image_rows.astype(jnp.float32).reshape(2, AZ_DEV, lines_dev)


def solution(mesh):
    in_specs = (
        P(None, ("pulse", "tile"), "range"),
        P(),
        P("range", None, None),
        P(("pulse", "tile"), None, "range"),
        P(("pulse", "tile"), None),
        P(("pulse", "tile")),
        P(("pulse", "tile")),
    )
    out_specs = P(None, ("tile", "pulse"), "range")
    return jax.shard_map(local, mesh=mesh, in_specs=in_specs, out_specs=out_specs, check_vma=False)
```

time: 324 us -> 198 us (0.61)
  blocking collectives: 155 us -> 89.8 us
  local copies, waits for them, and re-layouts: 61.7 us -> 15.7 us
  waiting for transfers between devices: 56.3 us -> 36.3 us
  starting transfers between devices: 6 us -> 24.2 us
  matrix products: 14.5 us -> 1.68 us
  Pallas kernels: 0 us -> 8.61 us
  other arithmetic: 13.9 us -> 8.01 us
    all_gather x2 -> x1, blocking collectives: 128 us -> 89.8 us  [local(): doppler_rows = lax.all_gather(doppler_rows, 'tile', axis=0, tiled=True)]
    unnamed x1 -> x0, blocking collectives: 26.6 us -> none
    reshape x36 -> x1, local copies, waits for them, and re-layouts: 22.1 us -> 0.09 us  [local(): jnp.where(visible != 0, targets, -(1 << 20))]
    another operation x68 -> x0, local copies, waits for them, and re-layouts: 21.6 us -> none  [toeplitz_block(): repeated = jnp.tile(segment, block_width)[:2 * block_width * block_width]]
    reduce_scatter x1, waiting for transfers between devices: 55.8 us -> 36.2 us  [local(): lax.psum_scatter(partial_image, 'pulse', scatter_dimension=0, tiled=True)]
    all_to_all x0 -> x1, starting transfers between devices: none -> 18.8 us  [local(): arrived = lax.all_to_all(steered, 'tile', 0, 0, tiled=True)]
    dot_general x20 -> x1, matrix products: 14.5 us -> 1.68 us  [local(): jnp.dot(factor, arrived, preferred_element_type=jnp.float32)]
    rev x0 -> x1, local copies, waits for them, and re-layouts: none -> 11.9 us  [skew_matrices(): jnp.flip(replica.astype(jnp.float32), 1)]
  transfers between devices with their start and end apart: 4 -> 4, of which waited for: 2 -> 1; matrix products, arithmetic and copies ran while one was open for 3% -> 10% of each run, Pallas kernels for 0% -> 1%
where the time goes in v1:
time: 198 us
  blocking collectives  89.8 us (45%)
  waiting for transfers between devices  36.3 us (18%)
  starting transfers between devices  24.2 us (12%)
  local copies, waits for them, and re-layouts  15.7 us (8%)
  between operations  13.5 us (7%)
  Pallas kernels  8.61 us (4%)
  other arithmetic  8.01 us (4%)
    all_gather x1, blocking collectives, local(): doppler_rows = lax.all_gather(doppler_rows, 'tile', axis=0, tiled=True)  89.8 us
    reduce_scatter x1, waiting for transfers between devices, local(): lax.psum_scatter(partial_image, 'pulse', scatter_dimension=0, tiled=True)  36.2 us
    all_to_all x1, starting transfers between devices, local(): arrived = lax.all_to_all(steered, 'tile', 0, 0, tiled=True)  18.8 us
    rev x1, local copies, waits for them, and re-layouts, skew_matrices(): jnp.flip(replica.astype(jnp.float32), 1)  11.9 us
    pallas_call x1, Pallas kernels, steered_values(): pl.pallas_call(steer_kernel, out_shape=jax.ShapeDtypeStruct((rows // puls...  6.87 us
    convert_element_type x1, other arithmetic, local(): factor = (jnp.cos(azimuth_angle) * norm_scale).astype(jnp.bfloat16)  4.55 us
    ppermute x1, starting transfers between devices, local(): left = lax.ppermute(echo[:, :, -half_chirp:], 'range', up)  4.03 us
  transfers between devices with their start and end apart: 4, of which 1 were waited for; matrix products, arithmetic and copies ran while one was open for 10% of the time, Pallas kernels for 1%

profile of v1, /device:TPU:1, one launch (start us, length us, event | category | flops | bytes accessed | tf_op | source)
XLA Modules:
  0.0 197.7 jit_solution(8621509521226349771)
XLA Ops:
  6.5 0.9 fusion.17
  7.4 4.0 %collective-permute-start = (bf16[2,8,2048]{2,1,0:T(8,128)(2,1)S(1)}, bf16[2,8,2048]{2,1,0:T(8,128)(2,1)S(1)}, u32[]{:S(2)}, u32[]{:S(2)}) collective-permute-start(bf16[2,8,2048]{2,1,0:T(8,128)(2,1)S(1)} %get-tuple-element.12), channel_id=1, source_target_pairs={{0,32},{32,64},{64,96},{1,33},{33,65},{65,97},{2,34},{34,66},{66,9... | collective-permute-start | bytes 196616 | tf_op jit(solution)/shard_map/ppermute | solution.py:148
  11.5 1.3 collective-permute-start.1
  12.8 0.9 fusion.9
  13.6 0.7 fusion.15
  14.4 11.9 %rev.4 = f32[2,4096]{1,0:T(2,128)S(1)} reverse(bf16[2,4096]{1,0:T(2,128)(2,1)} %param.8), dimensions={1} | reverse | bytes 49152 | tf_op jit(solution)/shard_map/jit(_flip)/rev | solution.py:31
  26.3 0.1 copy.11
  26.4 0.1 reshape.49.target_ref
  26.5 1.7 skew_matrices.1
  28.2 0.0 collective-permute-done.left_ref
  28.3 0.0 collective-permute-done.1.right_ref
  28.3 0.0 copy-start
  28.3 0.9 copy-done
  29.2 1.0 copy-done.1
  30.3 6.9 %steered_values.1 = bf16[32,16,1024]{2,1,0:T(8,128)(2,1)} custom-call(bf16[2,8,2048]{2,1,0:T(8,128)(2,1)S(1)} %collective-permute-done.left_ref, bf16[2,8,8192]{2,1,0:T(8,128)(2,1)S(1)} %copy-done, bf16[2,8,2048]{2,1,0:T(8,128)(2,1)S(1)} %collective-permute-done.1.right_ref, bf16[128,4224]{1,0:T(8,128)(2,1)S(1)} %get-tuple-element.8.real_ref, ...), custom_call_target="tpu_custom_call" | custom-call | flops 4000000000 | bytes 6291456 | tf_op jit(solution)/shard_map/steered_values/pallas_call | solution.py:117
  37.1 18.8 %all-to-all-start = ((bf16[32,16,1024]{2,1,0:T(8,128)(2,1)}), bf16[32,16,1024]{2,1,0:T(8,128)(2,1)S(1)}, u32[]{:S(2)}, u32[]{:S(2)}) async-start(bf16[32,16,1024]{2,1,0:T(8,128)(2,1)} %steered_values.1), calls=%async_computation | async-start | bytes 2097152 | tf_op jit(solution)/shard_map/all_to_all | solution.py:168
  55.9 0.0 reduce-scatter.2.cloned.1.call-start
  56.0 0.1 iota_add_fusion.1
  56.1 0.1 add.63
  56.2 0.1 broadcast_in_dim.12
  56.2 89.8 %all_gather.3 = s32[256,128]{1,0:T(8,128)S(1)} all-gather(s32[8,128]{1,0:T(8,128)S(1)} %broadcast_in_dim.12), channel_id=1, replica_groups=mesh['pulse'=4,'range'=4,'tile'=32] {'tile'}, dimensions={0}, use_global_device_ids=true | all-gather | bytes 135168 | tf_op jit(solution)/shard_map/all_gather | solution.py:153
  146.0 0.1 slice_reduce_fusion
  146.1 0.1 broadcast_in_dim.13
  146.2 0.1 mul.75
  146.3 0.1 sub.23
  146.4 0.1 sub.25
  146.5 4.6 %fusion.5 = bf16[512,512]{1,0:T(8,128)(2,1)S(1)} fusion(s32[512]{0:T(512)S(1)} %sub.25, s32[512]{0:T(512)S(1)} %sub.23, s32[512]{0:T(512)S(1)} %mul.75, s32[512]{0:T(512)S(1)} %add.63), kind=kLoop, calls=%fused_computation.9 | loop fusion | flops 4980736 | bytes 532480 | tf_op jit(solution)/shard_map/convert_element_type | solution.py:184
  151.1 0.0 all-to-all-done
  151.1 1.7 convolution_convert_fusion
  152.8 0.0 reduce-scatter.2.cloned.1.call-update
  152.8 36.2 %reduce-scatter.2.cloned.1.call-done = bf16[128,1024]{1,0:T(8,128)(2,1)} async-done(((bf16[512,1024]{1,0:T(8,128)(2,1)}), bf16[128,1024]{1,0:T(8,128)(2,1)}) %reduce-scatter.2.cloned.1.call-update) | async-done | bytes 262160 | tf_op jit(solution)/shard_map/reduce_scatter | solution.py:188
  189.0 1.8 convert.1
  (9 shorter events, 0.1 us)
Async XLA Ops:
  7.4 20.8 %collective-permute-start = (bf16[2,8,2048]{2,1,0:T(8,128)(2,1)S(1)}, bf16[2,8,2048]{2,1,0:T(8,128)(2,1)S(1)}, u32[]{:S(2)}, u32[]{:S(2)}) collective-permute-start(bf16[2,8,2048]{2,1,0:T(8,128)(2,1)S(1)} %get-tuple-element.12), channel_id=1, source_target_pairs={{0,32},{32,64},{64,96},{1,33},{33,65},{65,97},{2,34},{34,66},{66,9... | collective-permute-start | bytes 196616 | tf_op jit(solution)/shard_map/ppermute | solution.py:148
  11.5 16.8 %collective-permute-start.1 = (bf16[2,8,2048]{2,1,0:T(8,128)(2,1)S(1)}, bf16[2,8,2048]{2,1,0:T(8,128)(2,1)S(1)}, u32[]{:S(2)}, u32[]{:S(2)}) collective-permute-start(bf16[2,8,2048]{2,1,0:T(8,128)(2,1)S(1)} %get-tuple-element.11), channel_id=1, source_target_pairs={{32,0},{64,32},{96,64},{33,1},{65,33},{97,65},{34,2},{66,34},{98,6... | collective-permute-start | bytes 196616 | tf_op jit(solution)/shard_map/ppermute | solution.py:149
  28.3 1.0 copy-start
  29.2 1.0 copy-start.1
  37.1 19.0 %copy-start.2 = (s32[8]{0:T(128)S(1)}, s32[8]{0:T(128)}, u32[]{:S(2)}) copy-start(s32[8]{0:T(128)} %param.12) | copy-start | bytes 100
  37.1 114.0 %all-to-all-start = ((bf16[32,16,1024]{2,1,0:T(8,128)(2,1)}), bf16[32,16,1024]{2,1,0:T(8,128)(2,1)S(1)}, u32[]{:S(2)}, u32[]{:S(2)}) async-start(bf16[32,16,1024]{2,1,0:T(8,128)(2,1)} %steered_values.1), calls=%async_computation | async-start | bytes 2097152 | tf_op jit(solution)/shard_map/all_to_all | solution.py:168
  55.9 133.1 %reduce-scatter.2.cloned.1.call-start = ((), (), s32[]{:S(2)}) async-start(), calls=%async_computation.2 | async-start | bytes 1310720 | tf_op jit(solution)/shard_map/reduce_scatter | solution.py:188
Sparse Core Ops, SparseCore 0:
  152.9 36.0 reduce-scatter.1

commit v2 on v1

v2 whole, which is shorter than its diff:
```python
import functools
import math

import jax
import jax.numpy as jnp
from jax import lax
from jax.experimental import pallas as pl
from jax.experimental.pallas import tpu as pltpu
from jax.sharding import PartitionSpec as P

AZ_DEV = 64
LANES = 128
SUB = 8
GROUP = 8
DIGIT = 128
HIDDEN = 128
NOTE_STEP = 32
NOTE_BIN = 34
VMEM_LIMIT = 14 * 1024 * 1024

SINE = tuple((-1.0) ** n * (2.0 * math.pi) ** (2 * n + 1) / math.factorial(2 * n + 1) for n in range(8))


def cosine_of_turns(turns, total):
    away = jnp.abs(turns.astype(jnp.float32) * (1.0 / total) - 0.5) - 0.25
    square = away * away
    value = jnp.full_like(away, SINE[-1])
    for factor in SINE[-2::-1]:
        value = value * square + factor
    return value * away


def params(**extra):
    return pltpu.CompilerParams(vmem_limit_bytes=VMEM_LIMIT, **extra)


def pair_rows(first, second):
    return jnp.concatenate([first, second], axis=0).astype(jnp.bfloat16)


def block_cells(ref, block):
    place = slice(block * LANES, (block + 1) * LANES)
    return jnp.concatenate(
        [ref[0, :, place].astype(jnp.float32), ref[1, :, place].astype(jnp.float32)], axis=1
    )


def arrange(ref, even_ref, odd_ref):
    blocks = ref.shape[2] // LANES
    nothing = jnp.zeros((SUB, 2 * LANES), jnp.float32)
    for pair in range(blocks // 2):
        first = block_cells(ref, 2 * pair)
        second = block_cells(ref, 2 * pair + 1)
        third = block_cells(ref, 2 * pair + 2) if 2 * pair + 2 < blocks else nothing
        even_ref[pair] = pair_rows(first, second)
        odd_ref[pair] = pair_rows(second, third)


def rows_from(even_ref, odd_ref, first, count):
    source = even_ref if first % 2 == 0 else odd_ref
    pairs = (count + 1) // 2
    start = first // 2
    return source[start : start + pairs].reshape(pairs * 2 * SUB, 2 * LANES)


def turn_matrix(real_ref, imag_ref, minus_ref, turn):
    turns = real_ref.shape[1] // LANES
    place = slice((turns - 1 - turn) * LANES, (turns - turn) * LANES)
    upper = jnp.concatenate([real_ref[:, place], minus_ref[:, place]], axis=1)
    lower = jnp.concatenate([imag_ref[:, place], real_ref[:, place]], axis=1)
    return jnp.concatenate([upper, lower], axis=0)


def own_kernel(replica_ref, own_ref, real_ref, imag_ref, minus_ref, total_ref, flip_ref, even_ref, odd_ref):
    taps = replica_ref.shape[1] // LANES
    own_blocks = own_ref.shape[2] // LANES
    half = taps // 2
    row = lax.broadcasted_iota(jnp.int32, (LANES, LANES), 0)
    column = lax.broadcasted_iota(jnp.int32, (LANES, LANES), 1)
    mirror = jnp.where(row + column == LANES - 1, 1.0, 0.0).astype(jnp.bfloat16)
    pieces = [
        replica_ref[part : part + 1, block * LANES : (block + 1) * LANES].astype(jnp.float32)
        for part in range(2)
        for block in range(taps)
    ]
    stacked = jnp.concatenate(pieces, axis=0).astype(jnp.bfloat16)
    flip_ref[...] = jnp.dot(stacked, mirror, preferred_element_type=jnp.float32)
    nothing = jnp.zeros((1, LANES), jnp.float32)
    for part, target in ((0, real_ref), (1, imag_ref)):
        base = part * taps
        for block in range(taps + 1):
            before = flip_ref[base + taps - block : base + taps - block + 1] if block else nothing
            after = flip_ref[base + taps - 1 - block : base + taps - block] if block < taps else nothing
            wide = jnp.broadcast_to(jnp.concatenate([before, after], axis=1), (LANES, 2 * LANES))
            rolled = pltpu.roll(wide, 1, 1, stride=1, stride_axis=0)[:, LANES:]
            place = slice(block * LANES, (block + 1) * LANES)
            target[:, place] = rolled.astype(jnp.bfloat16)
            if part == 1:
                minus_ref[:, place] = (-rolled).astype(jnp.bfloat16)

    arrange(own_ref, even_ref, odd_ref)
    for turn in [half] + [t for t in range(taps + 1) if t != half]:
        matrix = turn_matrix(real_ref, imag_ref, minus_ref, turn)
        first_in = max(0, turn - half)
        first_out = max(0, half - turn)
        count = own_blocks - abs(turn - half)
        window = rows_from(even_ref, odd_ref, first_in, count)
        product = jnp.dot(window, matrix, preferred_element_type=jnp.float32)
        place = slice(first_out * SUB, (first_out + count) * SUB)
        if turn == half:
            total_ref[...] = product
        else:
            total_ref[place] += product[: count * SUB]


def own_part(replica, echo):
    taps = replica.shape[1]
    blocks = echo.shape[2] // LANES
    skewed = jax.ShapeDtypeStruct((LANES, taps + LANES), jnp.bfloat16)
    cells = pltpu.VMEM((blocks // 2, 2 * SUB, 2 * LANES), jnp.bfloat16)
    return pl.pallas_call(
        own_kernel,
        out_shape=(skewed, skewed, skewed, jax.ShapeDtypeStruct((blocks * SUB, 2 * LANES), jnp.float32)),
        scratch_shapes=[pltpu.VMEM((2 * taps // LANES, LANES), jnp.float32), cells, cells],
        name="own_part",
        compiler_params=params(),
        cost_estimate=pl.CostEstimate(flops=2000000000, bytes_accessed=8 * 1024 * 1024, transcendentals=0),
    )(replica, echo)


def edge_kernel(
    step_ref, bin_ref, left_ref, right_ref, real_ref, imag_ref, minus_ref, total_ref, band_ref, visible_ref,
    out_ref, sum_ref, even_ref, odd_ref, even2_ref, odd2_ref, note_ref,
):
    rows = total_ref.shape[0]
    own_blocks = rows // SUB
    half = left_ref.shape[2] // LANES
    arrange(left_ref, even_ref, odd_ref)
    arrange(right_ref, even2_ref, odd2_ref)
    sum_ref[...] = total_ref[...]
    for turn in range(half):
        matrix = turn_matrix(real_ref, imag_ref, minus_ref, turn)
        count = half - turn
        window = rows_from(even_ref, odd_ref, turn, count)
        product = jnp.dot(window, matrix, preferred_element_type=jnp.float32)
        sum_ref[: count * SUB] += product[: count * SUB]
    for turn in range(half + 1, 2 * half + 1):
        matrix = turn_matrix(real_ref, imag_ref, minus_ref, turn)
        count = turn - half
        window = rows_from(even2_ref, odd2_ref, 0, count)
        product = jnp.dot(window, matrix, preferred_element_type=jnp.float32)
        sum_ref[(own_blocks - count) * SUB :] += product[: count * SUB]
    out_ref[:rows] = sum_ref[...].astype(jnp.bfloat16)
    pulse = lax.broadcasted_iota(jnp.int32, (SUB, LANES), 0)
    lane = lax.broadcasted_iota(jnp.int32, (SUB, LANES), 1)
    note = jnp.zeros((SUB, LANES), jnp.int32)
    for index in range(SUB):
        step = step_ref[index]
        bin_here = bin_ref[index]
        for at, digit in enumerate((step // DIGIT, step % DIGIT, bin_here // DIGIT, bin_here % DIGIT)):
            note = jnp.where((pulse == index) & (lane == NOTE_STEP + at), digit, note)
    note_ref[...] = note.astype(jnp.float32)
    bands = jnp.where(visible_ref[...] != 0, band_ref[...] // LANES, HIDDEN)
    note_ref[:, : bands.shape[1]] = bands.astype(jnp.float32)
    nothing = jnp.zeros((SUB, LANES), jnp.float32)
    out_ref[rows:, :LANES] = pair_rows(note_ref[...], nothing)
    out_ref[rows:, LANES:] = pair_rows(nothing, nothing)


def edge_part(left, right, skewed, total, bands, visible, steps, bins):
    half = left.shape[2] // LANES
    cells = pltpu.VMEM((half // 2, 2 * SUB, 2 * LANES), jnp.bfloat16)
    rows = total.shape[0]
    return pl.pallas_call(
        edge_kernel,
        out_shape=jax.ShapeDtypeStruct((rows + 2 * SUB, 2 * LANES), jnp.bfloat16),
        in_specs=[pl.BlockSpec(memory_space=pltpu.SMEM)] * 2 + [pl.BlockSpec(memory_space=pltpu.VMEM)] * 8,
        scratch_shapes=[pltpu.VMEM(total.shape, jnp.float32), cells, cells, cells, cells]
        + [pltpu.VMEM((SUB, LANES), jnp.float32)],
        name="edge_part",
        compiler_params=params(),
        cost_estimate=pl.CostEstimate(flops=300000000, bytes_accessed=4 * 1024 * 1024, transcendentals=0),
    )(steps, bins, left, right, *skewed, total, bands, visible)


def steer_kernel(lines_total, hops, *refs):
    chunk_refs, (interp_ref, out_ref, band_ref) = refs[:-3], refs[-3:]
    line_blocks = interp_ref.shape[0]
    lines = line_blocks * LANES
    far = lax.axis_size("tile") // GROUP
    group = lax.rem(lax.axis_index("tile") // GROUP + hops, far)
    first_line = lax.axis_index("range") * lines
    note_rows = 2 * SUB
    rows = GROUP * SUB
    for chunk, parts in enumerate(chunk_refs):
        whole = parts[...]
        count = whole.shape[0] - note_rows
        compressed = whole[:count]
        note = whole[count:].astype(jnp.float32)[:SUB, :LANES]
        lane = lax.broadcasted_iota(jnp.int32, (SUB, LANES), 1)

        def pick(index):
            return jnp.sum(jnp.where(lane == index, note, 0.0), axis=1, keepdims=True).astype(jnp.int32)

        pulse = lax.broadcasted_iota(jnp.int32, (SUB, 1), 0)
        wanted = jnp.concatenate([pick(group * GROUP + tile) * SUB + pulse for tile in range(GROUP)], axis=0)
        column = lax.broadcasted_iota(jnp.int32, (rows, count), 1)
        away = column - wanted
        for piece in range(line_blocks + 1):
            chooser = jnp.where(away == piece * SUB, 1.0, 0.0).astype(jnp.bfloat16)
            picked = jnp.dot(chooser, compressed, preferred_element_type=jnp.float32)
            band_ref[piece] = picked.astype(jnp.bfloat16)

        step = pick(NOTE_STEP) * DIGIT + pick(NOTE_STEP + 1)
        number = first_line + lax.broadcasted_iota(jnp.int32, (SUB, lines), 1)
        turns = (step * number) & (lines_total - 1)
        cosine = cosine_of_turns(turns, lines_total)
        sine = cosine_of_turns((turns - lines_total // 4) & (lines_total - 1), lines_total)

        for line in range(line_blocks):
            both = []
            for part in range(2):
                half = slice(part * LANES, (part + 1) * LANES)
                both.append(jnp.concatenate([band_ref[line, :, half], band_ref[line + 1, :, half]], axis=1))
            values = jnp.dot(
                jnp.concatenate(both, axis=0), interp_ref[line], preferred_element_type=jnp.float32
            )
            real = values[:rows].reshape(GROUP, SUB, LANES)
            imag = values[rows:].reshape(GROUP, SUB, LANES)
            at = slice(line * LANES, (line + 1) * LANES)
            cos_here = cosine[:, at][None]
            sin_here = sine[:, at][None]
            steered = jnp.concatenate(
                [real * cos_here - imag * sin_here, real * sin_here + imag * cos_here], axis=1
            )
            out_ref[:, chunk * 2 * SUB : (chunk + 1) * 2 * SUB, at] = steered.astype(jnp.bfloat16)
        tail = jnp.concatenate([note, note], axis=0).astype(jnp.bfloat16)
        out_ref[:, chunk * 2 * SUB : (chunk + 1) * 2 * SUB, lines:] = jnp.broadcast_to(
            tail[None], (GROUP, 2 * SUB, LANES)
        )


def steer_part(chunks, interp, lines_total, hops):
    line_blocks = interp.shape[0]
    lines = line_blocks * LANES
    return pl.pallas_call(
        functools.partial(steer_kernel, lines_total, hops),
        out_shape=jax.ShapeDtypeStruct((GROUP, len(chunks) * 2 * SUB, lines + LANES), jnp.bfloat16),
        scratch_shapes=[pltpu.VMEM((line_blocks + 1, GROUP * SUB, 2 * LANES), jnp.bfloat16)],
        name="steer_part",
        compiler_params=params(),
        cost_estimate=pl.CostEstimate(
            flops=20000000000 * len(chunks), bytes_accessed=1024, transcendentals=0
        ),
    )(*chunks, interp)


def image_kernel(total, scale, first, last, values_ref, *refs):
    rows = values_ref.shape[0] * values_ref.shape[1]
    lines = values_ref.shape[2] - LANES
    note = values_ref[:, :, lines:].reshape(rows, LANES).astype(jnp.float32)
    turned = note.T
    bins = turned[NOTE_BIN : NOTE_BIN + 1] * DIGIT + turned[NOTE_BIN + 1 : NOTE_BIN + 2]
    bins = bins.astype(jnp.int32)
    in_part = (lax.broadcasted_iota(jnp.int32, (1, rows), 1) // SUB) & 1
    groups = lax.axis_size("pulse")
    first_line = lax.axis_index("tile") * (groups * AZ_DEV)
    me = lax.axis_index("pulse")
    block = 2 * AZ_DEV
    index = lax.broadcasted_iota(jnp.int32, (block, 1), 0)
    out_part = index // AZ_DEV
    values = values_ref[:, :, :lines].reshape(rows, lines)
    if first:
        outs = refs
    else:
        before_ref, outs = refs[0], refs[1:]
    for hop in range(groups):
        owner = lax.rem(me + hop, groups)
        line = first_line + owner * AZ_DEV + index % AZ_DEV
        turns = (line * bins + (in_part - out_part) * (total // 4)) & (total - 1)
        factor = (cosine_of_turns(turns, total) * scale).astype(jnp.bfloat16)
        image = jnp.dot(factor, values, preferred_element_type=jnp.float32)
        if not first:
            image = image + before_ref[hop]
        if not last:
            outs[0][hop] = image
        elif hop == 0:
            outs[0][...] = image
        else:
            outs[hop][...] = image.astype(jnp.bfloat16)


def image_part(values, before, last, total, scale):
    groups = lax.axis_size("pulse")
    lines = values.shape[2] - LANES
    block = 2 * AZ_DEV
    if last:
        out_shape = (jax.ShapeDtypeStruct((block, lines), jnp.float32),) + tuple(
            jax.ShapeDtypeStruct((block, lines), jnp.bfloat16) for _ in range(groups - 1)
        )
    else:
        out_shape = jax.ShapeDtypeStruct((groups, block, lines), jnp.float32)
    operands = (values,) + (() if before is None else (before,))
    return pl.pallas_call(
        functools.partial(image_kernel, total, scale, before is None, last),
        out_shape=out_shape,
        name="image_part",
        compiler_params=params(),
        cost_estimate=pl.CostEstimate(flops=20000000000, bytes_accessed=1024, transcendentals=0),
    )(*operands)


def local(echo, replica, interp, band_start, visible, doppler, range_step):
    half_chirp = replica.shape[1] // 2
    pulses_dev = echo.shape[1]
    lines_dev = interp.shape[0] * interp.shape[2]
    tile_count = lax.axis_size("tile")
    pulse_count = lax.axis_size("pulse")
    range_count = lax.axis_size("range")
    range_total = lines_dev * range_count
    azimuth_total = AZ_DEV * pulse_count * tile_count
    norm_scale = (pulses_dev * pulse_count * tile_count) ** (-0.5)
    far = tile_count // GROUP

    up = [(i, i + 1) for i in range(range_count - 1)]
    down = [(i + 1, i) for i in range(range_count - 1)]
    left = lax.ppermute(echo[:, :, -half_chirp:], "range", up)
    right = lax.ppermute(echo[:, :, :half_chirp], "range", down)
    *skewed, total = own_part(replica, echo)

    bands = band_start.reshape(pulses_dev, tile_count)
    mine = edge_part(left, right, skewed, total, bands, visible, range_step, doppler)

    def group_shift(hops):
        return [
            (h * GROUP + i, (h + hops) % far * GROUP + i) for h in range(far) for i in range(GROUP)
        ]

    groups = [[h * GROUP + i for i in range(GROUP)] for h in range(far)]

    def steer(chunks, hops=0):
        return steer_part(chunks, interp, range_total, hops)

    def exchange(steered):
        return lax.all_to_all(steered, "tile", 0, 0, axis_index_groups=groups, tiled=True)

    def add_image(values, before, last=False):
        return image_part(values, before, last, azimuth_total, norm_scale)

    below = lax.ppermute(mine, "tile", group_shift(1))
    above = lax.ppermute(mine, "tile", group_shift(-1))
    steered = steer([mine], far // 2)
    opposite = lax.ppermute(exchange(steered), "tile", group_shift(far // 2))
    mine, _ = lax.optimization_barrier((mine, steered))
    image = add_image(exchange(steer([mine])), None)
    image = add_image(exchange(steer([below, above])), image)
    image = add_image(opposite, image, last=True)

    kept, *sent = image
    for hop, cells in enumerate(sent, 1):
        pairs = [(i, (i + hop) % pulse_count) for i in range(pulse_count)]
        kept = kept + lax.ppermute(cells, "pulse", pairs).astype(jnp.float32)
    return kept.reshape(2, AZ_DEV, lines_dev)


def solution(mesh):
    in_specs = (
        P(None, ("pulse", "tile"), "range"),
        P(),
        P("range", None, None),
        P(("pulse", "tile"), None, "range"),
        P(("pulse", "tile"), None),
        P(("pulse", "tile")),
        P(("pulse", "tile")),
    )
    out_specs = P(None, ("tile", "pulse"), "range")
    return jax.shard_map(local, mesh=mesh, in_specs=in_specs, out_specs=out_specs, check_vma=False)
```

time: 198 us -> 109 us (0.55)
  the two profiles are of different devices: /device:TPU:1 before, /device:TPU:240 now
where the time goes in v2:
time: 109 us; the launch traced here: 108 us
  starting transfers between devices  55.4 us (51%)
  waiting for transfers between devices  34.6 us (32%)
  Pallas kernels  11.4 us (10%)
  local copies, waits for them, and re-layouts  5.48 us (5%)
    ppermute x3, starting transfers between devices, local(): kept = kept + lax.ppermute(cells, 'pulse', pairs).astype(jnp.float32)  19.2 us
    ppermute x3, waiting for transfers between devices, local(): kept = kept + lax.ppermute(cells, 'pulse', pairs).astype(jnp.float32)  19.1 us
    all_to_all x3, waiting for transfers between devices, exchange(): lax.all_to_all(steered, 'tile', 0, 0, axis_index_groups=groups, tiled=True)  15.5 us
    all_to_all x3, starting transfers between devices, exchange(): lax.all_to_all(steered, 'tile', 0, 0, axis_index_groups=groups, tiled=True)  12.4 us
    ppermute x1, starting transfers between devices, local(): opposite = lax.ppermute(exchange(steered), 'tile', group_shift(far // 2))  8.25 us
    ppermute x1, starting transfers between devices, local(): below = lax.ppermute(mine, 'tile', group_shift(1))  7.83 us
    pallas_call x3, Pallas kernels, steer_part(): pl.pallas_call(functools.partial(steer_kernel, lines_total, hops), out_sh...  5.4 us
    unnamed x18, local copies, waits for them, and re-layouts  4.6 us
  transfers between devices with their start and end apart: 11, of which 4 were waited for; matrix products, arithmetic and copies ran while one was open for 0% of the time, Pallas kernels for 9%

profile of v2, /device:TPU:240, one launch (start us, length us, event | category | flops | bytes accessed | tf_op | source)
XLA Modules:
  0.0 108.0 jit_solution(4020314175435086227)
XLA Ops:
  0.0 0.9 fusion
  0.9 2.4 %collective-permute-start.1 = (bf16[2,8,2048]{2,1,0:T(8,128)(2,1)S(1)}, bf16[2,8,2048]{2,1,0:T(8,128)(2,1)S(1)}, u32[]{:S(2)}, u32[]{:S(2)}) collective-permute-start(bf16[2,8,2048]{2,1,0:T(8,128)(2,1)S(1)} %get-tuple-element.23), channel_id=1, source_target_pairs={{32,0},{64,32},{96,64},{33,1},{65,33},{97,65},{34,2},{66,34},{98,6... | collective-permute-start | bytes 196616 | tf_op jit(solution)/shard_map/ppermute | solution.py:328
  3.2 3.5 %collective-permute-start = (bf16[2,8,2048]{2,1,0:T(8,128)(2,1)S(1)}, bf16[2,8,2048]{2,1,0:T(8,128)(2,1)S(1)}, u32[]{:S(2)}, u32[]{:S(2)}) collective-permute-start(bf16[2,8,2048]{2,1,0:T(8,128)(2,1)S(1)} %get-tuple-element.24), channel_id=1, source_target_pairs={{0,32},{32,64},{64,96},{1,33},{33,65},{65,97},{2,34},{34,66},{66,9... | collective-permute-start | bytes 196616 | tf_op jit(solution)/shard_map/ppermute | solution.py:327
  6.7 0.0 copy-start
  6.8 0.9 copy-done
  7.7 0.7 copy-done.6
  8.4 2.7 %own_part.1 = (bf16[128,4224]{1,0:T(8,128)(2,1)S(1)}, bf16[128,4224]{1,0:T(8,128)(2,1)S(1)}, bf16[128,4224]{1,0:T(8,128)(2,1)S(1)}, f32[512,256]{1,0:T(8,128)S(1)}) custom-call(bf16[2,4096]{1,0:T(2,128)(2,1)S(1)} %copy-done.6, bf16[2,8,8192]{2,1,0:T(8,128)(2,1)S(1)} %copy-done), custom_call_target="tpu_custom_call" | custom-call | flops 2000000000 | bytes 8388608 | tf_op jit(solution)/shard_map/own_part/pallas_call | solution.py:121
  11.1 0.0 collective-permute-done.1.right_ref
  11.1 0.0 copy-start.5
  11.2 1.4 %edge_part.1.refs_0_ = bf16[528,256]{1,0:T(8,128)(2,1)S(1)} custom-call(s32[8]{0:T(128)S(1)} %copy-done.3, s32[8]{0:T(128)S(1)} %copy-done.4, bf16[2,8,2048]{2,1,0:T(8,128)(2,1)S(1)} %collective-permute-done.left_ref, bf16[2,8,2048]{2,1,0:T(8,128)(2,1)S(1)} %collective-permute-done.1.right_ref, bf16[128,4224]{1,0:T(8,128)(2,1)S(1)} %get-tuple-element.14.real_ref, ...), custom_call_target="tpu_custom_call" | custom-call | flops 300000000 | bytes 4194304 | tf_op jit(solution)/shard_map/edge_part/pallas_call | solution.py:174
  12.5 1.9 %collective-permute-start.4 = (bf16[528,256]{1,0:T(8,128)(2,1)S(1)}, bf16[528,256]{1,0:T(8,128)(2,1)S(1)}, u32[]{:S(2)}, u32[]{:S(2)}) collective-permute-start(bf16[528,256]{1,0:T(8,128)(2,1)S(1)} %edge_part.1.refs_0_), channel_id=1, source_target_pairs={{0,24},{1,25},{2,26},{3,27},{4,28},{5,29},{6,30},{7,31},{8,0},{9,1... | collective-permute-start | bytes 811016 | tf_op jit(solution)/shard_map/ppermute | solution.py:351
  14.4 7.8 %collective-permute-start.3 = (bf16[528,256]{1,0:T(8,128)(2,1)S(1)}, bf16[528,256]{1,0:T(8,128)(2,1)S(1)}, u32[]{:S(2)}, u32[]{:S(2)}) collective-permute-start(bf16[528,256]{1,0:T(8,128)(2,1)S(1)} %edge_part.1.refs_0_), channel_id=1, source_target_pairs={{0,8},{1,9},{2,10},{3,11},{4,12},{5,13},{6,14},{7,15},{8,16},{9,17... | collective-permute-start | bytes 811016 | tf_op jit(solution)/shard_map/ppermute | solution.py:350
  22.3 1.6 %steer_part.3 = bf16[8,16,1152]{2,1,0:T(8,128)(2,1)} custom-call(bf16[528,256]{1,0:T(8,128)(2,1)S(1)} %edge_part.1.refs_0_, bf16[8,256,128]{2,1,0:T(8,128)(2,1)S(1)} %copy-done.5), custom_call_target="tpu_custom_call" | custom-call | flops 20000000000 | bytes 1024 | tf_op jit(solution)/shard_map/steer_part/pallas_call | solution.py:246
  23.9 4.3 %all-to-all-start = ((bf16[8,16,1152]{2,1,0:T(8,128)(2,1)}), bf16[8,16,1152]{2,1,0:T(8,128)(2,1)S(1)}, u32[]{:S(2)}, u32[]{:S(2)}) async-start(bf16[8,16,1152]{2,1,0:T(8,128)(2,1)} %steer_part.3), calls=%async_computation | async-start | bytes 589824 | tf_op jit(solution)/shard_map/all_to_all | solution.py:345
  28.2 1.6 %steer_part.5 = bf16[8,16,1152]{2,1,0:T(8,128)(2,1)} custom-call(bf16[528,256]{1,0:T(8,128)(2,1)S(1)} %edge_part.1.refs_0_, bf16[8,256,128]{2,1,0:T(8,128)(2,1)S(1)} %copy-done.5), custom_call_target="tpu_custom_call" | custom-call | flops 20000000000 | bytes 1024 | tf_op jit(solution)/shard_map/steer_part/pallas_call | solution.py:246
  29.7 6.3 %all-to-all-done = bf16[8,16,1152]{2,1,0:T(8,128)(2,1)S(1)} async-done(((bf16[8,16,1152]{2,1,0:T(8,128)(2,1)}), bf16[8,16,1152]{2,1,0:T(8,128)(2,1)S(1)}, u32[]{:S(2)}, u32[]{:S(2)}) %all-to-all-start) | async-done | bytes 294944 | tf_op jit(solution)/shard_map/all_to_all | solution.py:345
  36.1 3.4 %all-to-all-start.2 = ((bf16[8,16,1152]{2,1,0:T(8,128)(2,1)}), bf16[8,16,1152]{2,1,0:T(8,128)(2,1)S(1)}, u32[]{:S(2)}, u32[]{:S(2)}) async-start(bf16[8,16,1152]{2,1,0:T(8,128)(2,1)} %steer_part.5), calls=%async_computation.2 | async-start | bytes 589824 | tf_op jit(solution)/shard_map/all_to_all | solution.py:345
  39.5 8.2 %collective-permute-start.2 = (bf16[8,16,1152]{2,1,0:T(8,128)(2,1)S(1)}, bf16[8,16,1152]{2,1,0:T(8,128)(2,1)S(1)}, u32[]{:S(2)}, u32[]{:S(2)}) collective-permute-start(bf16[8,16,1152]{2,1,0:T(8,128)(2,1)S(1)} %all-to-all-done), channel_id=1, source_target_pairs={{0,16},{1,17},{2,18},{3,19},{4,20},{5,21},{6,22},{7,23},{8,24},{9,... | collective-permute-start | bytes 884744 | tf_op jit(solution)/shard_map/ppermute | solution.py:353
  47.8 2.3 %steer_part.4 = bf16[8,32,1152]{2,1,0:T(8,128)(2,1)} custom-call(bf16[528,256]{1,0:T(8,128)(2,1)S(1)} %collective-permute-done.3.refs_0_, bf16[528,256]{1,0:T(8,128)(2,1)S(1)} %collective-permute-done.4.refs_1_, bf16[8,256,128]{2,1,0:T(8,128)(2,1)S(1)} %copy-done.5), custom_call_target="tpu_custom_call" | custom-call | flops 40000000000 | bytes 1024 | tf_op jit(solution)/shard_map/steer_part/pallas_call | solution.py:246
  50.0 4.7 %all-to-all-start.1 = ((bf16[8,32,1152]{2,1,0:T(8,128)(2,1)}), bf16[8,32,1152]{2,1,0:T(8,128)(2,1)S(1)}, u32[]{:S(2)}, u32[]{:S(2)}) async-start(bf16[8,32,1152]{2,1,0:T(8,128)(2,1)} %steer_part.4), calls=%async_computation.1 | async-start | bytes 1179648 | tf_op jit(solution)/shard_map/all_to_all | solution.py:345
  54.7 0.5 image_part.3.refs_0_
  55.3 1.3 %copy-done.7 = f32[4,128,1024]{2,1,0:T(8,128)} copy-done((f32[4,128,1024]{2,1,0:T(8,128)}, f32[4,128,1024]{2,1,0:T(8,128)S(1)}, u32[]{:S(2)}) %copy-start.7) | copy-done | bytes 2097176
  56.6 9.2 %all-to-all-done.1.values_ref = bf16[8,32,1152]{2,1,0:T(8,128)(2,1)S(1)} async-done(((bf16[8,32,1152]{2,1,0:T(8,128)(2,1)}), bf16[8,32,1152]{2,1,0:T(8,128)(2,1)S(1)}, u32[]{:S(2)}, u32[]{:S(2)}) %all-to-all-start.1) | async-done | bytes 589856 | tf_op jit(solution)/shard_map/all_to_all | solution.py:345
  65.8 1.6 %copy-done.8 = f32[4,128,1024]{2,1,0:T(8,128)S(1)} copy-done((f32[4,128,1024]{2,1,0:T(8,128)S(1)}, f32[4,128,1024]{2,1,0:T(8,128)}, u32[]{:S(2)}) %copy-start.8) | copy-done | bytes 2097176
  67.3 0.9 image_part.4.refs_0_
  68.2 0.6 image_part.5
  68.8 9.6 %collective-permute-start.5 = (bf16[128,1024]{1,0:T(8,128)(2,1)S(1)}, bf16[128,1024]{1,0:T(8,128)(2,1)S(1)}, u32[]{:S(2)}, u32[]{:S(2)}) collective-permute-start(bf16[128,1024]{1,0:T(8,128)(2,1)S(1)} %get-tuple-element.20), channel_id=1, source_target_pairs={{0,128},{128,256},{256,384},{384,0},{1,129},{129,257},{257,385},{3... | collective-permute-start | bytes 786440 | tf_op jit(solution)/shard_map/ppermute | solution.py:362
  78.4 7.6 %collective-permute-start.6 = (bf16[128,1024]{1,0:T(8,128)(2,1)S(1)}, bf16[128,1024]{1,0:T(8,128)(2,1)S(1)}, u32[]{:S(2)}, u32[]{:S(2)}) collective-permute-start(bf16[128,1024]{1,0:T(8,128)(2,1)S(1)} %get-tuple-element.21), channel_id=1, source_target_pairs={{0,256},{128,384},{256,0},{384,128},{1,257},{129,385},{257,1},{385... | collective-permute-start | bytes 786440 | tf_op jit(solution)/shard_map/ppermute | solution.py:362
  86.1 1.9 %collective-permute-start.7 = (bf16[128,1024]{1,0:T(8,128)(2,1)S(1)}, bf16[128,1024]{1,0:T(8,128)(2,1)S(1)}, u32[]{:S(2)}, u32[]{:S(2)}) collective-permute-start(bf16[128,1024]{1,0:T(8,128)(2,1)S(1)} %get-tuple-element.22), channel_id=1, source_target_pairs={{0,384},{128,0},{256,128},{384,256},{1,385},{129,1},{257,129},{385... | collective-permute-start | bytes 786440 | tf_op jit(solution)/shard_map/ppermute | solution.py:362
  88.0 1.1 %collective-permute-done.5 = bf16[128,1024]{1,0:T(8,128)(2,1)S(1)} collective-permute-done((bf16[128,1024]{1,0:T(8,128)(2,1)S(1)}, bf16[128,1024]{1,0:T(8,128)(2,1)S(1)}, u32[]{:S(2)}, u32[]{:S(2)}) %collective-permute-start.5) | collective-permute-done | bytes 262176 | tf_op jit(solution)/shard_map/ppermute | solution.py:362
  89.1 18.0 %collective-permute-done.6 = bf16[128,1024]{1,0:T(8,128)(2,1)S(1)} collective-permute-done((bf16[128,1024]{1,0:T(8,128)(2,1)S(1)}, bf16[128,1024]{1,0:T(8,128)(2,1)S(1)}, u32[]{:S(2)}, u32[]{:S(2)}) %collective-permute-start.6) | collective-permute-done | bytes 262176 | tf_op jit(solution)/shard_map/ppermute | solution.py:362
  107.1 0.9 convert_add_fusion
  (18 shorter events, 0.0 us)
Async XLA Ops:
  0.9 10.2 %collective-permute-start.1 = (bf16[2,8,2048]{2,1,0:T(8,128)(2,1)S(1)}, bf16[2,8,2048]{2,1,0:T(8,128)(2,1)S(1)}, u32[]{:S(2)}, u32[]{:S(2)}) collective-permute-start(bf16[2,8,2048]{2,1,0:T(8,128)(2,1)S(1)} %get-tuple-element.23), channel_id=1, source_target_pairs={{32,0},{64,32},{96,64},{33,1},{65,33},{97,65},{34,2},{66,34},{98,6... | collective-permute-start | bytes 196616 | tf_op jit(solution)/shard_map/ppermute | solution.py:328
  3.2 7.8 %collective-permute-start = (bf16[2,8,2048]{2,1,0:T(8,128)(2,1)S(1)}, bf16[2,8,2048]{2,1,0:T(8,128)(2,1)S(1)}, u32[]{:S(2)}, u32[]{:S(2)}) collective-permute-start(bf16[2,8,2048]{2,1,0:T(8,128)(2,1)S(1)} %get-tuple-element.24), channel_id=1, source_target_pairs={{0,32},{32,64},{64,96},{1,33},{33,65},{65,97},{2,34},{34,66},{66,9... | collective-permute-start | bytes 196616 | tf_op jit(solution)/shard_map/ppermute | solution.py:327
  6.7 1.0 copy-start
  7.7 0.7 copy-start.6
  8.4 2.7 %copy-start.1 = (s32[8,32,1]{1,2,0:T(1,128)S(1)}, s32[8,32,1]{1,2,0:T(1,128)}, u32[]{:S(2)}) copy-start(s32[8,32,1]{1,2,0:T(1,128)} %param.10) | copy-start | bytes 3076
  8.4 2.7 %copy-start.2 = (s32[8,32]{1,0:T(8,128)S(1)}, s32[8,32]{1,0:T(8,128)}, u32[]{:S(2)}) copy-start(s32[8,32]{1,0:T(8,128)} %visible_ref.1) | copy-start | bytes 3076
  8.4 2.7 %copy-start.3 = (s32[8]{0:T(128)S(1)}, s32[8]{0:T(128)}, u32[]{:S(2)}) copy-start(s32[8]{0:T(128)} %step_ref.1) | copy-start | bytes 100
  8.4 2.7 %copy-start.4 = (s32[8]{0:T(128)S(1)}, s32[8]{0:T(128)}, u32[]{:S(2)}) copy-start(s32[8]{0:T(128)} %bin_ref.1) | copy-start | bytes 100
  11.1 11.1 %copy-start.5 = (bf16[8,256,128]{2,1,0:T(8,128)(2,1)S(1)}, bf16[8,256,128]{2,1,0:T(8,128)(2,1)}, u32[]{:S(2)}) copy-start(bf16[8,256,128]{2,1,0:T(8,128)(2,1)} %refs_1_.3) | copy-start | bytes 1572868
  12.5 35.2 %collective-permute-start.4 = (bf16[528,256]{1,0:T(8,128)(2,1)S(1)}, bf16[528,256]{1,0:T(8,128)(2,1)S(1)}, u32[]{:S(2)}, u32[]{:S(2)}) collective-permute-start(bf16[528,256]{1,0:T(8,128)(2,1)S(1)} %edge_part.1.refs_0_), channel_id=1, source_target_pairs={{0,24},{1,25},{2,26},{3,27},{4,28},{5,29},{6,30},{7,31},{8,0},{9,1... | collective-permute-start | bytes 811016 | tf_op jit(solution)/shard_map/ppermute | solution.py:351
  14.4 33.3 %collective-permute-start.3 = (bf16[528,256]{1,0:T(8,128)(2,1)S(1)}, bf16[528,256]{1,0:T(8,128)(2,1)S(1)}, u32[]{:S(2)}, u32[]{:S(2)}) collective-permute-start(bf16[528,256]{1,0:T(8,128)(2,1)S(1)} %edge_part.1.refs_0_), channel_id=1, source_target_pairs={{0,8},{1,9},{2,10},{3,11},{4,12},{5,13},{6,14},{7,15},{8,16},{9,17... | collective-permute-start | bytes 811016 | tf_op jit(solution)/shard_map/ppermute | solution.py:350
  23.9 12.2 %all-to-all-start = ((bf16[8,16,1152]{2,1,0:T(8,128)(2,1)}), bf16[8,16,1152]{2,1,0:T(8,128)(2,1)S(1)}, u32[]{:S(2)}, u32[]{:S(2)}) async-start(bf16[8,16,1152]{2,1,0:T(8,128)(2,1)} %steer_part.3), calls=%async_computation | async-start | bytes 589824 | tf_op jit(solution)/shard_map/all_to_all | solution.py:345
  36.1 14.0 %all-to-all-start.2 = ((bf16[8,16,1152]{2,1,0:T(8,128)(2,1)}), bf16[8,16,1152]{2,1,0:T(8,128)(2,1)S(1)}, u32[]{:S(2)}, u32[]{:S(2)}) async-start(bf16[8,16,1152]{2,1,0:T(8,128)(2,1)} %steer_part.5), calls=%async_computation.2 | async-start | bytes 589824 | tf_op jit(solution)/shard_map/all_to_all | solution.py:345
  39.5 28.7 %collective-permute-start.2 = (bf16[8,16,1152]{2,1,0:T(8,128)(2,1)S(1)}, bf16[8,16,1152]{2,1,0:T(8,128)(2,1)S(1)}, u32[]{:S(2)}, u32[]{:S(2)}) collective-permute-start(bf16[8,16,1152]{2,1,0:T(8,128)(2,1)S(1)} %all-to-all-done), channel_id=1, source_target_pairs={{0,16},{1,17},{2,18},{3,19},{4,20},{5,21},{6,22},{7,23},{8,24},{9,... | collective-permute-start | bytes 884744 | tf_op jit(solution)/shard_map/ppermute | solution.py:353
  50.0 15.7 %all-to-all-start.1 = ((bf16[8,32,1152]{2,1,0:T(8,128)(2,1)}), bf16[8,32,1152]{2,1,0:T(8,128)(2,1)S(1)}, u32[]{:S(2)}, u32[]{:S(2)}) async-start(bf16[8,32,1152]{2,1,0:T(8,128)(2,1)} %steer_part.4), calls=%async_computation.1 | async-start | bytes 1179648 | tf_op jit(solution)/shard_map/all_to_all | solution.py:345
  55.2 1.3 %copy-start.7 = (f32[4,128,1024]{2,1,0:T(8,128)}, f32[4,128,1024]{2,1,0:T(8,128)S(1)}, u32[]{:S(2)}) copy-start(f32[4,128,1024]{2,1,0:T(8,128)S(1)} %image_part.3.refs_0_) | copy-start | bytes 6291460
  65.8 1.6 %copy-start.8 = (f32[4,128,1024]{2,1,0:T(8,128)S(1)}, f32[4,128,1024]{2,1,0:T(8,128)}, u32[]{:S(2)}) copy-start(f32[4,128,1024]{2,1,0:T(8,128)} %copy-done.7) | copy-start | bytes 6291460
  68.8 20.3 %collective-permute-start.5 = (bf16[128,1024]{1,0:T(8,128)(2,1)S(1)}, bf16[128,1024]{1,0:T(8,128)(2,1)S(1)}, u32[]{:S(2)}, u32[]{:S(2)}) collective-permute-start(bf16[128,1024]{1,0:T(8,128)(2,1)S(1)} %get-tuple-element.20), channel_id=1, source_target_pairs={{0,128},{128,256},{256,384},{384,0},{1,129},{129,257},{257,385},{3... | collective-permute-start | bytes 786440 | tf_op jit(solution)/shard_map/ppermute | solution.py:362
  78.4 28.7 %collective-permute-start.6 = (bf16[128,1024]{1,0:T(8,128)(2,1)S(1)}, bf16[128,1024]{1,0:T(8,128)(2,1)S(1)}, u32[]{:S(2)}, u32[]{:S(2)}) collective-permute-start(bf16[128,1024]{1,0:T(8,128)(2,1)S(1)} %get-tuple-element.21), channel_id=1, source_target_pairs={{0,256},{128,384},{256,0},{384,128},{1,257},{129,385},{257,1},{385... | collective-permute-start | bytes 786440 | tf_op jit(solution)/shard_map/ppermute | solution.py:362
  86.1 21.0 %collective-permute-start.7 = (bf16[128,1024]{1,0:T(8,128)(2,1)S(1)}, bf16[128,1024]{1,0:T(8,128)(2,1)S(1)}, u32[]{:S(2)}, u32[]{:S(2)}) collective-permute-start(bf16[128,1024]{1,0:T(8,128)(2,1)S(1)} %get-tuple-element.22), channel_id=1, source_target_pairs={{0,384},{128,0},{256,128},{384,256},{1,385},{129,1},{257,129},{385... | collective-permute-start | bytes 786440 | tf_op jit(solution)/shard_map/ppermute | solution.py:362

commit v3 on v2

--- a/solution.py
+++ b/solution.py
@@ -17,6 +17,8 @@
 NOTE_STEP = 32
 NOTE_BIN = 34
 VMEM_LIMIT = 14 * 1024 * 1024
+IMAGE_COST = 20000000000
+STEER_COST = 20000000000
 
 SINE = tuple((-1.0) ** n * (2.0 * math.pi) ** (2 * n + 1) / math.factorial(2 * n + 1) for n in range(8))
 
@@ -183,12 +185,11 @@
     )(steps, bins, left, right, *skewed, total, bands, visible)
 
 
-def steer_kernel(lines_total, hops, *refs):
+def steer_kernel(lines_total, group_hops, *refs):
     chunk_refs, (interp_ref, out_ref, band_ref) = refs[:-3], refs[-3:]
     line_blocks = interp_ref.shape[0]
     lines = line_blocks * LANES
     far = lax.axis_size("tile") // GROUP
-    group = lax.rem(lax.axis_index("tile") // GROUP + hops, far)
     first_line = lax.axis_index("range") * lines
     note_rows = 2 * SUB
     rows = GROUP * SUB
@@ -196,6 +197,7 @@
         whole = parts[...]
         count = whole.shape[0] - note_rows
         compressed = whole[:count]
+        group = lax.rem(lax.axis_index("tile") // GROUP + group_hops[chunk], far)
         note = whole[count:].astype(jnp.float32)[:SUB, :LANES]
         lane = lax.broadcasted_iota(jnp.int32, (SUB, LANES), 1)
 
@@ -240,48 +242,53 @@
         )
 
 
-def steer_part(chunks, interp, lines_total, hops):
+def steer_part(chunks, interp, lines_total, group_hops):
     line_blocks = interp.shape[0]
     lines = line_blocks * LANES
     return pl.pallas_call(
-        functools.partial(steer_kernel, lines_total, hops),
+        functools.partial(steer_kernel, lines_total, tuple(group_hops)),
         out_shape=jax.ShapeDtypeStruct((GROUP, len(chunks) * 2 * SUB, lines + LANES), jnp.bfloat16),
         scratch_shapes=[pltpu.VMEM((line_blocks + 1, GROUP * SUB, 2 * LANES), jnp.bfloat16)],
         name="steer_part",
         compiler_params=params(),
         cost_estimate=pl.CostEstimate(
-            flops=20000000000 * len(chunks), bytes_accessed=1024, transcendentals=0
+            flops=STEER_COST * len(chunks), bytes_accessed=1024, transcendentals=0
         ),
     )(*chunks, interp)
 
 
-def image_kernel(total, scale, first, last, values_ref, *refs):
-    rows = values_ref.shape[0] * values_ref.shape[1]
-    lines = values_ref.shape[2] - LANES
-    note = values_ref[:, :, lines:].reshape(rows, LANES).astype(jnp.float32)
-    turned = note.T
+def azimuth_factor(total, scale, note, hop):
+    rows = note.shape[0]
+    turned = note.astype(jnp.float32).T
     bins = turned[NOTE_BIN : NOTE_BIN + 1] * DIGIT + turned[NOTE_BIN + 1 : NOTE_BIN + 2]
     bins = bins.astype(jnp.int32)
     in_part = (lax.broadcasted_iota(jnp.int32, (1, rows), 1) // SUB) & 1
     groups = lax.axis_size("pulse")
-    first_line = lax.axis_index("tile") * (groups * AZ_DEV)
-    me = lax.axis_index("pulse")
-    block = 2 * AZ_DEV
-    index = lax.broadcasted_iota(jnp.int32, (block, 1), 0)
+    index = lax.broadcasted_iota(jnp.int32, (2 * AZ_DEV, 1), 0)
     out_part = index // AZ_DEV
-    values = values_ref[:, :, :lines].reshape(rows, lines)
+    owner = lax.rem(lax.axis_index("pulse") + hop, groups)
+    line = lax.axis_index("tile") * (groups * AZ_DEV) + owner * AZ_DEV + index % AZ_DEV
+    turns = (line * bins + (in_part - out_part) * (total // 4)) & (total - 1)
+    return (cosine_of_turns(turns, total) * scale).astype(jnp.bfloat16)
+
+
+def image_kernel(total, scale, windows, first, last, *refs):
+    count = len(windows)
+    value_refs = refs[:count]
     if first:
-        outs = refs
+        outs = refs[count:]
     else:
-        before_ref, outs = refs[0], refs[1:]
-    for hop in range(groups):
-        owner = lax.rem(me + hop, groups)
-        line = first_line + owner * AZ_DEV + index % AZ_DEV
-        turns = (line * bins + (in_part - out_part) * (total // 4)) & (total - 1)
-        factor = (cosine_of_turns(turns, total) * scale).astype(jnp.bfloat16)
-        image = jnp.dot(factor, values, preferred_element_type=jnp.float32)
-        if not first:
-            image = image + before_ref[hop]
+        before_ref, outs = refs[count], refs[count + 1 :]
+    for hop in range(lax.axis_size("pulse")):
+        image = None if first else before_ref[hop]
+        for value_ref, pulse_rows in zip(value_refs, windows):
+            rows = value_ref.shape[0] * pulse_rows
+            lines = value_ref.shape[2] - LANES
+            note = value_ref[:, :pulse_rows, lines:].reshape(rows, LANES)
+            values = value_ref[:, :pulse_rows, :lines].reshape(rows, lines)
+            factor = azimuth_factor(total, scale, note, hop)
+            added = jnp.dot(factor, values, preferred_element_type=jnp.float32)
+            image = added if image is None else image + added
         if not last:
             outs[0][hop] = image
         elif hop == 0:
@@ -290,9 +297,9 @@
             outs[hop][...] = image.astype(jnp.bfloat16)
 
 
-def image_part(values, before, last, total, scale):
+def image_part(values, before, last, total, scale, windows):
     groups = lax.axis_size("pulse")
-    lines = values.shape[2] - LANES
+    lines = values[0].shape[2] - LANES
     block = 2 * AZ_DEV
     if last:
         out_shape = (jax.ShapeDtypeStruct((block, lines), jnp.float32),) + tuple(
@@ -300,13 +307,13 @@
         )
     else:
         out_shape = jax.ShapeDtypeStruct((groups, block, lines), jnp.float32)
-    operands = (values,) + (() if before is None else (before,))
+    operands = tuple(values) + (() if before is None else (before,))
     return pl.pallas_call(
-        functools.partial(image_kernel, total, scale, before is None, last),
+        functools.partial(image_kernel, total, scale, tuple(windows), before is None, last),
         out_shape=out_shape,
         name="image_part",
         compiler_params=params(),
-        cost_estimate=pl.CostEstimate(flops=20000000000, bytes_accessed=1024, transcendentals=0),
+        cost_estimate=pl.CostEstimate(flops=IMAGE_COST, bytes_accessed=1024, transcendentals=0),
     )(*operands)
 
 
@@ -338,26 +345,30 @@
 
     groups = [[h * GROUP + i for i in range(GROUP)] for h in range(far)]
 
-    def steer(chunks, hops=0):
-        return steer_part(chunks, interp, range_total, hops)
+    def steer(chunks, group_hops):
+        return steer_part(chunks, interp, range_total, group_hops)
 
     def exchange(steered):
         return lax.all_to_all(steered, "tile", 0, 0, axis_index_groups=groups, tiled=True)
 
-    def add_image(values, before, last=False):
-        return image_part(values, before, last, azimuth_total, norm_scale)
+    def add_image(values, before, last=False, windows=None):
+        windows = windows or [v.shape[1] for v in values]
+        return image_part(values, before, last, azimuth_total, norm_scale, windows)
 
     below = lax.ppermute(mine, "tile", group_shift(1))
     above = lax.ppermute(mine, "tile", group_shift(-1))
-    steered = steer([mine], far // 2)
+    steered = steer([mine], [far // 2])
     opposite = lax.ppermute(exchange(steered), "tile", group_shift(far // 2))
     mine, _ = lax.optimization_barrier((mine, steered))
-    image = add_image(exchange(steer([mine])), None)
-    image = add_image(exchange(steer([below, above])), image)
-    image = add_image(opposite, image, last=True)
+    own = exchange(steer([mine], [0]))
+    near = exchange(steer([below, above], [0, 0]))
+    image = add_image([own], None)
+    image = add_image([near], image)
+    image = add_image([opposite], image, last=True)
 
     kept, *sent = image
-    for hop, cells in enumerate(sent, 1):
+    for hop in (2, 3, 1):
+        cells = sent[hop - 1]
         pairs = [(i, (i + hop) % pulse_count) for i in range(pulse_count)]
         kept = kept + lax.ppermute(cells, "pulse", pairs).astype(jnp.float32)
     return kept.reshape(2, AZ_DEV, lines_dev)

time: 109 us -> 108 us (level)
  the two profiles are of different devices: /device:TPU:240 before, /device:TPU:81 now
where the time goes in v3:
time: 108 us; the launch traced here: 107 us
  starting transfers between devices  52.6 us (49%)
  waiting for transfers between devices  36.9 us (34%)
  Pallas kernels  11.4 us (11%)
  local copies, waits for them, and re-layouts  5.48 us (5%)
    ppermute x3, waiting for transfers between devices, local(): kept = kept + lax.ppermute(cells, 'pulse', pairs).astype(jnp.float32)  18.5 us
    all_to_all x3, starting transfers between devices, exchange(): lax.all_to_all(steered, 'tile', 0, 0, axis_index_groups=groups, tiled=True)  15 us
    all_to_all x3, waiting for transfers between devices, exchange(): lax.all_to_all(steered, 'tile', 0, 0, axis_index_groups=groups, tiled=True)  13.8 us
    ppermute x1, starting transfers between devices, local(): above = lax.ppermute(mine, 'tile', group_shift(-1))  10.7 us
    ppermute x1, starting transfers between devices, local(): opposite = lax.ppermute(exchange(steered), 'tile', group_shift(far // 2))  10.5 us
    ppermute x3, starting transfers between devices, local(): kept = kept + lax.ppermute(cells, 'pulse', pairs).astype(jnp.float32)  9.13 us
    pallas_call x3, Pallas kernels, steer_part(): pl.pallas_call(functools.partial(steer_kernel, lines_total, tuple(group_h...  5.4 us
    unnamed x18, local copies, waits for them, and re-layouts  4.6 us
  transfers between devices with their start and end apart: 11, of which 6 were waited for; matrix products, arithmetic and copies ran while one was open for 0% of the time, Pallas kernels for 9%

profile of v3, /device:TPU:81, one launch (start us, length us, event | category | flops | bytes accessed | tf_op | source)
XLA Modules:
  0.0 107.5 jit_solution(17186126736216460959)
XLA Ops:
  0.0 0.9 fusion
  0.9 2.1 %collective-permute-start.1 = (bf16[2,8,2048]{2,1,0:T(8,128)(2,1)S(1)}, bf16[2,8,2048]{2,1,0:T(8,128)(2,1)S(1)}, u32[]{:S(2)}, u32[]{:S(2)}) collective-permute-start(bf16[2,8,2048]{2,1,0:T(8,128)(2,1)S(1)} %get-tuple-element.23), channel_id=1, source_target_pairs={{32,0},{64,32},{96,64},{33,1},{65,33},{97,65},{34,2},{66,34},{98,6... | collective-permute-start | bytes 196616 | tf_op jit(solution)/shard_map/ppermute | solution.py:335
  3.0 3.2 %collective-permute-start = (bf16[2,8,2048]{2,1,0:T(8,128)(2,1)S(1)}, bf16[2,8,2048]{2,1,0:T(8,128)(2,1)S(1)}, u32[]{:S(2)}, u32[]{:S(2)}) collective-permute-start(bf16[2,8,2048]{2,1,0:T(8,128)(2,1)S(1)} %get-tuple-element.24), channel_id=1, source_target_pairs={{0,32},{32,64},{64,96},{1,33},{33,65},{65,97},{2,34},{34,66},{66,9... | collective-permute-start | bytes 196616 | tf_op jit(solution)/shard_map/ppermute | solution.py:334
  6.2 0.0 copy-start
  6.2 0.9 copy-done
  7.1 0.7 copy-done.6
  7.9 2.7 %own_part.1 = (bf16[128,4224]{1,0:T(8,128)(2,1)S(1)}, bf16[128,4224]{1,0:T(8,128)(2,1)S(1)}, bf16[128,4224]{1,0:T(8,128)(2,1)S(1)}, f32[512,256]{1,0:T(8,128)S(1)}) custom-call(bf16[2,4096]{1,0:T(2,128)(2,1)S(1)} %copy-done.6, bf16[2,8,8192]{2,1,0:T(8,128)(2,1)S(1)} %copy-done), custom_call_target="tpu_custom_call" | custom-call | flops 2000000000 | bytes 8388608 | tf_op jit(solution)/shard_map/own_part/pallas_call | solution.py:123
  10.6 1.4 %edge_part.1.refs_0_ = bf16[528,256]{1,0:T(8,128)(2,1)S(1)} custom-call(s32[8]{0:T(128)S(1)} %copy-done.3, s32[8]{0:T(128)S(1)} %copy-done.4, bf16[2,8,2048]{2,1,0:T(8,128)(2,1)S(1)} %collective-permute-done.left_ref, bf16[2,8,2048]{2,1,0:T(8,128)(2,1)S(1)} %collective-permute-done.1.right_ref, bf16[128,4224]{1,0:T(8,128)(2,1)S(1)} %get-tuple-element.14.real_ref, ...), custom_call_target="tpu_custom_call" | custom-call | flops 300000000 | bytes 4194304 | tf_op jit(solution)/shard_map/edge_part/pallas_call | solution.py:176
  12.0 10.7 %collective-permute-start.4 = (bf16[528,256]{1,0:T(8,128)(2,1)S(1)}, bf16[528,256]{1,0:T(8,128)(2,1)S(1)}, u32[]{:S(2)}, u32[]{:S(2)}) collective-permute-start(bf16[528,256]{1,0:T(8,128)(2,1)S(1)} %edge_part.1.refs_0_), channel_id=1, source_target_pairs={{0,24},{1,25},{2,26},{3,27},{4,28},{5,29},{6,30},{7,31},{8,0},{9,1... | collective-permute-start | bytes 811016 | tf_op jit(solution)/shard_map/ppermute | solution.py:359
  22.6 1.9 %collective-permute-start.3 = (bf16[528,256]{1,0:T(8,128)(2,1)S(1)}, bf16[528,256]{1,0:T(8,128)(2,1)S(1)}, u32[]{:S(2)}, u32[]{:S(2)}) collective-permute-start(bf16[528,256]{1,0:T(8,128)(2,1)S(1)} %edge_part.1.refs_0_), channel_id=1, source_target_pairs={{0,8},{1,9},{2,10},{3,11},{4,12},{5,13},{6,14},{7,15},{8,16},{9,17... | collective-permute-start | bytes 811016 | tf_op jit(solution)/shard_map/ppermute | solution.py:358
  24.6 1.6 %steer_part.3 = bf16[8,16,1152]{2,1,0:T(8,128)(2,1)} custom-call(bf16[528,256]{1,0:T(8,128)(2,1)S(1)} %edge_part.1.refs_0_, bf16[8,256,128]{2,1,0:T(8,128)(2,1)S(1)} %copy-done.5), custom_call_target="tpu_custom_call" | custom-call | flops 20000000000 | bytes 1024 | tf_op jit(solution)/shard_map/steer_part/pallas_call | solution.py:248
  26.1 5.8 %all-to-all-start = ((bf16[8,16,1152]{2,1,0:T(8,128)(2,1)}), bf16[8,16,1152]{2,1,0:T(8,128)(2,1)S(1)}, u32[]{:S(2)}, u32[]{:S(2)}) async-start(bf16[8,16,1152]{2,1,0:T(8,128)(2,1)} %steer_part.3), calls=%async_computation | async-start | bytes 589824 | tf_op jit(solution)/shard_map/all_to_all | solution.py:352
  32.0 1.6 %steer_part.5 = bf16[8,16,1152]{2,1,0:T(8,128)(2,1)} custom-call(bf16[528,256]{1,0:T(8,128)(2,1)S(1)} %edge_part.1.refs_0_, bf16[8,256,128]{2,1,0:T(8,128)(2,1)S(1)} %copy-done.5), custom_call_target="tpu_custom_call" | custom-call | flops 20000000000 | bytes 1024 | tf_op jit(solution)/shard_map/steer_part/pallas_call | solution.py:248
  33.5 5.5 %all-to-all-done = bf16[8,16,1152]{2,1,0:T(8,128)(2,1)S(1)} async-done(((bf16[8,16,1152]{2,1,0:T(8,128)(2,1)}), bf16[8,16,1152]{2,1,0:T(8,128)(2,1)S(1)}, u32[]{:S(2)}, u32[]{:S(2)}) %all-to-all-start) | async-done | bytes 294944 | tf_op jit(solution)/shard_map/all_to_all | solution.py:352
  39.1 4.1 %all-to-all-start.2 = ((bf16[8,16,1152]{2,1,0:T(8,128)(2,1)}), bf16[8,16,1152]{2,1,0:T(8,128)(2,1)S(1)}, u32[]{:S(2)}, u32[]{:S(2)}) async-start(bf16[8,16,1152]{2,1,0:T(8,128)(2,1)} %steer_part.5), calls=%async_computation.2 | async-start | bytes 589824 | tf_op jit(solution)/shard_map/all_to_all | solution.py:352
  43.2 10.5 %collective-permute-start.2 = (bf16[8,16,1152]{2,1,0:T(8,128)(2,1)S(1)}, bf16[8,16,1152]{2,1,0:T(8,128)(2,1)S(1)}, u32[]{:S(2)}, u32[]{:S(2)}) collective-permute-start(bf16[8,16,1152]{2,1,0:T(8,128)(2,1)S(1)} %all-to-all-done), channel_id=1, source_target_pairs={{0,16},{1,17},{2,18},{3,19},{4,20},{5,21},{6,22},{7,23},{8,24},{9,... | collective-permute-start | bytes 884744 | tf_op jit(solution)/shard_map/ppermute | solution.py:361
  53.7 2.2 %steer_part.4 = bf16[8,32,1152]{2,1,0:T(8,128)(2,1)} custom-call(bf16[528,256]{1,0:T(8,128)(2,1)S(1)} %collective-permute-done.3.refs_0_, bf16[528,256]{1,0:T(8,128)(2,1)S(1)} %collective-permute-done.4.refs_1_, bf16[8,256,128]{2,1,0:T(8,128)(2,1)S(1)} %copy-done.5), custom_call_target="tpu_custom_call" | custom-call | flops 40000000000 | bytes 1024 | tf_op jit(solution)/shard_map/steer_part/pallas_call | solution.py:248
  56.0 5.1 %all-to-all-start.1 = ((bf16[8,32,1152]{2,1,0:T(8,128)(2,1)}), bf16[8,32,1152]{2,1,0:T(8,128)(2,1)S(1)}, u32[]{:S(2)}, u32[]{:S(2)}) async-start(bf16[8,32,1152]{2,1,0:T(8,128)(2,1)} %steer_part.4), calls=%async_computation.1 | async-start | bytes 1179648 | tf_op jit(solution)/shard_map/all_to_all | solution.py:352
  61.1 0.5 image_part.3.refs_1_
  61.6 1.3 %copy-done.7 = f32[4,128,1024]{2,1,0:T(8,128)} copy-done((f32[4,128,1024]{2,1,0:T(8,128)}, f32[4,128,1024]{2,1,0:T(8,128)S(1)}, u32[]{:S(2)}) %copy-start.7) | copy-done | bytes 2097176
  63.0 8.3 %all-to-all-done.1.refs_0_ = bf16[8,32,1152]{2,1,0:T(8,128)(2,1)S(1)} async-done(((bf16[8,32,1152]{2,1,0:T(8,128)(2,1)}), bf16[8,32,1152]{2,1,0:T(8,128)(2,1)S(1)}, u32[]{:S(2)}, u32[]{:S(2)}) %all-to-all-start.1) | async-done | bytes 589856 | tf_op jit(solution)/shard_map/all_to_all | solution.py:352
  71.3 1.6 %copy-done.8 = f32[4,128,1024]{2,1,0:T(8,128)S(1)} copy-done((f32[4,128,1024]{2,1,0:T(8,128)S(1)}, f32[4,128,1024]{2,1,0:T(8,128)}, u32[]{:S(2)}) %copy-start.8) | copy-done | bytes 2097176
  72.9 0.9 image_part.4.refs_1_
  73.7 4.6 %collective-permute-done.2.refs_0_ = bf16[8,16,1152]{2,1,0:T(8,128)(2,1)S(1)} collective-permute-done((bf16[8,16,1152]{2,1,0:T(8,128)(2,1)S(1)}, bf16[8,16,1152]{2,1,0:T(8,128)(2,1)S(1)}, u32[]{:S(2)}, u32[]{:S(2)}) %collective-permute-start.2) | collective-permute-done | bytes 294944 | tf_op jit(solution)/shard_map/ppermute | solution.py:361
  78.3 0.6 image_part.5
  78.9 1.9 %collective-permute-start.5 = (bf16[128,1024]{1,0:T(8,128)(2,1)S(1)}, bf16[128,1024]{1,0:T(8,128)(2,1)S(1)}, u32[]{:S(2)}, u32[]{:S(2)}) collective-permute-start(bf16[128,1024]{1,0:T(8,128)(2,1)S(1)} %get-tuple-element.20), channel_id=1, source_target_pairs={{0,256},{128,384},{256,0},{384,128},{1,257},{129,385},{257,1},{385... | collective-permute-start | bytes 786440 | tf_op jit(solution)/shard_map/ppermute | solution.py:373
  80.8 4.1 %collective-permute-start.6 = (bf16[128,1024]{1,0:T(8,128)(2,1)S(1)}, bf16[128,1024]{1,0:T(8,128)(2,1)S(1)}, u32[]{:S(2)}, u32[]{:S(2)}) collective-permute-start(bf16[128,1024]{1,0:T(8,128)(2,1)S(1)} %get-tuple-element.21), channel_id=1, source_target_pairs={{0,384},{128,0},{256,128},{384,256},{1,385},{129,1},{257,129},{385... | collective-permute-start | bytes 786440 | tf_op jit(solution)/shard_map/ppermute | solution.py:373
  85.0 3.1 %collective-permute-start.7 = (bf16[128,1024]{1,0:T(8,128)(2,1)S(1)}, bf16[128,1024]{1,0:T(8,128)(2,1)S(1)}, u32[]{:S(2)}, u32[]{:S(2)}) collective-permute-start(bf16[128,1024]{1,0:T(8,128)(2,1)S(1)} %get-tuple-element.22), channel_id=1, source_target_pairs={{0,128},{128,256},{256,384},{384,0},{1,129},{129,257},{257,385},{3... | collective-permute-start | bytes 786440 | tf_op jit(solution)/shard_map/ppermute | solution.py:373
  88.1 2.2 %collective-permute-done.5 = bf16[128,1024]{1,0:T(8,128)(2,1)S(1)} collective-permute-done((bf16[128,1024]{1,0:T(8,128)(2,1)S(1)}, bf16[128,1024]{1,0:T(8,128)(2,1)S(1)}, u32[]{:S(2)}, u32[]{:S(2)}) %collective-permute-start.5) | collective-permute-done | bytes 262176 | tf_op jit(solution)/shard_map/ppermute | solution.py:373
  90.3 12.8 %collective-permute-done.6 = bf16[128,1024]{1,0:T(8,128)(2,1)S(1)} collective-permute-done((bf16[128,1024]{1,0:T(8,128)(2,1)S(1)}, bf16[128,1024]{1,0:T(8,128)(2,1)S(1)}, u32[]{:S(2)}, u32[]{:S(2)}) %collective-permute-start.6) | collective-permute-done | bytes 262176 | tf_op jit(solution)/shard_map/ppermute | solution.py:373
  103.1 3.4 %collective-permute-done.7 = bf16[128,1024]{1,0:T(8,128)(2,1)S(1)} collective-permute-done((bf16[128,1024]{1,0:T(8,128)(2,1)S(1)}, bf16[128,1024]{1,0:T(8,128)(2,1)S(1)}, u32[]{:S(2)}, u32[]{:S(2)}) %collective-permute-start.7) | collective-permute-done | bytes 262176 | tf_op jit(solution)/shard_map/ppermute | solution.py:373
  106.5 0.9 convert_add_fusion
  (18 shorter events, 0.0 us)
Async XLA Ops:
  0.9 9.6 %collective-permute-start.1 = (bf16[2,8,2048]{2,1,0:T(8,128)(2,1)S(1)}, bf16[2,8,2048]{2,1,0:T(8,128)(2,1)S(1)}, u32[]{:S(2)}, u32[]{:S(2)}) collective-permute-start(bf16[2,8,2048]{2,1,0:T(8,128)(2,1)S(1)} %get-tuple-element.23), channel_id=1, source_target_pairs={{32,0},{64,32},{96,64},{33,1},{65,33},{97,65},{34,2},{66,34},{98,6... | collective-permute-start | bytes 196616 | tf_op jit(solution)/shard_map/ppermute | solution.py:335
  3.0 7.6 %collective-permute-start = (bf16[2,8,2048]{2,1,0:T(8,128)(2,1)S(1)}, bf16[2,8,2048]{2,1,0:T(8,128)(2,1)S(1)}, u32[]{:S(2)}, u32[]{:S(2)}) collective-permute-start(bf16[2,8,2048]{2,1,0:T(8,128)(2,1)S(1)} %get-tuple-element.24), channel_id=1, source_target_pairs={{0,32},{32,64},{64,96},{1,33},{33,65},{65,97},{2,34},{34,66},{66,9... | collective-permute-start | bytes 196616 | tf_op jit(solution)/shard_map/ppermute | solution.py:334
  6.2 1.0 copy-start
  7.1 0.7 copy-start.6
  7.9 2.7 %copy-start.1 = (s32[8,32,1]{1,2,0:T(1,128)S(1)}, s32[8,32,1]{1,2,0:T(1,128)}, u32[]{:S(2)}) copy-start(s32[8,32,1]{1,2,0:T(1,128)} %param.10) | copy-start | bytes 3076
  7.9 2.7 %copy-start.2 = (s32[8,32]{1,0:T(8,128)S(1)}, s32[8,32]{1,0:T(8,128)}, u32[]{:S(2)}) copy-start(s32[8,32]{1,0:T(8,128)} %visible_ref.1) | copy-start | bytes 3076
  7.9 2.7 %copy-start.3 = (s32[8]{0:T(128)S(1)}, s32[8]{0:T(128)}, u32[]{:S(2)}) copy-start(s32[8]{0:T(128)} %step_ref.1) | copy-start | bytes 100
  7.9 2.7 %copy-start.4 = (s32[8]{0:T(128)S(1)}, s32[8]{0:T(128)}, u32[]{:S(2)}) copy-start(s32[8]{0:T(128)} %bin_ref.1) | copy-start | bytes 100
  10.6 14.0 %copy-start.5 = (bf16[8,256,128]{2,1,0:T(8,128)(2,1)S(1)}, bf16[8,256,128]{2,1,0:T(8,128)(2,1)}, u32[]{:S(2)}) copy-start(bf16[8,256,128]{2,1,0:T(8,128)(2,1)} %refs_1_.3) | copy-start | bytes 1572868
  12.0 41.8 %collective-permute-start.4 = (bf16[528,256]{1,0:T(8,128)(2,1)S(1)}, bf16[528,256]{1,0:T(8,128)(2,1)S(1)}, u32[]{:S(2)}, u32[]{:S(2)}) collective-permute-start(bf16[528,256]{1,0:T(8,128)(2,1)S(1)} %edge_part.1.refs_0_), channel_id=1, source_target_pairs={{0,24},{1,25},{2,26},{3,27},{4,28},{5,29},{6,30},{7,31},{8,0},{9,1... | collective-permute-start | bytes 811016 | tf_op jit(solution)/shard_map/ppermute | solution.py:359
  22.6 31.1 %collective-permute-start.3 = (bf16[528,256]{1,0:T(8,128)(2,1)S(1)}, bf16[528,256]{1,0:T(8,128)(2,1)S(1)}, u32[]{:S(2)}, u32[]{:S(2)}) collective-permute-start(bf16[528,256]{1,0:T(8,128)(2,1)S(1)} %edge_part.1.refs_0_), channel_id=1, source_target_pairs={{0,8},{1,9},{2,10},{3,11},{4,12},{5,13},{6,14},{7,15},{8,16},{9,17... | collective-permute-start | bytes 811016 | tf_op jit(solution)/shard_map/ppermute | solution.py:358
  26.1 12.9 %all-to-all-start = ((bf16[8,16,1152]{2,1,0:T(8,128)(2,1)}), bf16[8,16,1152]{2,1,0:T(8,128)(2,1)S(1)}, u32[]{:S(2)}, u32[]{:S(2)}) async-start(bf16[8,16,1152]{2,1,0:T(8,128)(2,1)} %steer_part.3), calls=%async_computation | async-start | bytes 589824 | tf_op jit(solution)/shard_map/all_to_all | solution.py:352
  39.1 16.9 %all-to-all-start.2 = ((bf16[8,16,1152]{2,1,0:T(8,128)(2,1)}), bf16[8,16,1152]{2,1,0:T(8,128)(2,1)S(1)}, u32[]{:S(2)}, u32[]{:S(2)}) async-start(bf16[8,16,1152]{2,1,0:T(8,128)(2,1)} %steer_part.5), calls=%async_computation.2 | async-start | bytes 589824 | tf_op jit(solution)/shard_map/all_to_all | solution.py:352
  43.2 35.2 %collective-permute-start.2 = (bf16[8,16,1152]{2,1,0:T(8,128)(2,1)S(1)}, bf16[8,16,1152]{2,1,0:T(8,128)(2,1)S(1)}, u32[]{:S(2)}, u32[]{:S(2)}) collective-permute-start(bf16[8,16,1152]{2,1,0:T(8,128)(2,1)S(1)} %all-to-all-done), channel_id=1, source_target_pairs={{0,16},{1,17},{2,18},{3,19},{4,20},{5,21},{6,22},{7,23},{8,24},{9,... | collective-permute-start | bytes 884744 | tf_op jit(solution)/shard_map/ppermute | solution.py:361
  56.0 15.3 %all-to-all-start.1 = ((bf16[8,32,1152]{2,1,0:T(8,128)(2,1)}), bf16[8,32,1152]{2,1,0:T(8,128)(2,1)S(1)}, u32[]{:S(2)}, u32[]{:S(2)}) async-start(bf16[8,32,1152]{2,1,0:T(8,128)(2,1)} %steer_part.4), calls=%async_computation.1 | async-start | bytes 1179648 | tf_op jit(solution)/shard_map/all_to_all | solution.py:352
  61.6 1.3 %copy-start.7 = (f32[4,128,1024]{2,1,0:T(8,128)}, f32[4,128,1024]{2,1,0:T(8,128)S(1)}, u32[]{:S(2)}) copy-start(f32[4,128,1024]{2,1,0:T(8,128)S(1)} %image_part.3.refs_1_) | copy-start | bytes 6291460
  71.3 1.6 %copy-start.8 = (f32[4,128,1024]{2,1,0:T(8,128)S(1)}, f32[4,128,1024]{2,1,0:T(8,128)}, u32[]{:S(2)}) copy-start(f32[4,128,1024]{2,1,0:T(8,128)} %copy-done.7) | copy-start | bytes 6291460
  78.9 11.4 %collective-permute-start.5 = (bf16[128,1024]{1,0:T(8,128)(2,1)S(1)}, bf16[128,1024]{1,0:T(8,128)(2,1)S(1)}, u32[]{:S(2)}, u32[]{:S(2)}) collective-permute-start(bf16[128,1024]{1,0:T(8,128)(2,1)S(1)} %get-tuple-element.20), channel_id=1, source_target_pairs={{0,256},{128,384},{256,0},{384,128},{1,257},{129,385},{257,1},{385... | collective-permute-start | bytes 786440 | tf_op jit(solution)/shard_map/ppermute | solution.py:373
  80.8 22.3 %collective-permute-start.6 = (bf16[128,1024]{1,0:T(8,128)(2,1)S(1)}, bf16[128,1024]{1,0:T(8,128)(2,1)S(1)}, u32[]{:S(2)}, u32[]{:S(2)}) collective-permute-start(bf16[128,1024]{1,0:T(8,128)(2,1)S(1)} %get-tuple-element.21), channel_id=1, source_target_pairs={{0,384},{128,0},{256,128},{384,256},{1,385},{129,1},{257,129},{385... | collective-permute-start | bytes 786440 | tf_op jit(solution)/shard_map/ppermute | solution.py:373
  85.0 21.6 %collective-permute-start.7 = (bf16[128,1024]{1,0:T(8,128)(2,1)S(1)}, bf16[128,1024]{1,0:T(8,128)(2,1)S(1)}, u32[]{:S(2)}, u32[]{:S(2)}) collective-permute-start(bf16[128,1024]{1,0:T(8,128)(2,1)S(1)} %get-tuple-element.22), channel_id=1, source_target_pairs={{0,128},{128,256},{256,384},{384,0},{1,129},{129,257},{257,385},{3... | collective-permute-start | bytes 786440 | tf_op jit(solution)/shard_map/ppermute | solution.py:373

commit v4 on v3

--- a/solution.py
+++ b/solution.py
@@ -367,7 +367,7 @@
     image = add_image([opposite], image, last=True)
 
     kept, *sent = image
-    for hop in (2, 3, 1):
+    for hop in (2, 1, 3):
         cells = sent[hop - 1]
         pairs = [(i, (i + hop) % pulse_count) for i in range(pulse_count)]
         kept = kept + lax.ppermute(cells, "pulse", pairs).astype(jnp.float32)

time: 108 us -> 108 us (level)
  transfers between devices with their start and end apart: 11 -> 11, of which waited for: 6 -> 5; matrix products, arithmetic and copies ran while one was open for 0% -> 0% of each run, Pallas kernels for 9% -> 9%
where the time goes in v4:
time: 108 us; the launch traced here: 107 us
  starting transfers between devices  52.6 us (49%)
  waiting for transfers between devices  36.9 us (34%)
  Pallas kernels  11.4 us (11%)
  local copies, waits for them, and re-layouts  5.48 us (5%)
    ppermute x3, waiting for transfers between devices, local(): kept = kept + lax.ppermute(cells, 'pulse', pairs).astype(jnp.float32)  18.5 us
    all_to_all x3, starting transfers between devices, exchange(): lax.all_to_all(steered, 'tile', 0, 0, axis_index_groups=groups, tiled=True)  15 us
    all_to_all x3, waiting for transfers between devices, exchange(): lax.all_to_all(steered, 'tile', 0, 0, axis_index_groups=groups, tiled=True)  13.8 us
    ppermute x1, starting transfers between devices, local(): above = lax.ppermute(mine, 'tile', group_shift(-1))  10.7 us
    ppermute x1, starting transfers between devices, local(): opposite = lax.ppermute(exchange(steered), 'tile', group_shift(far // 2))  10.5 us
    ppermute x3, starting transfers between devices, local(): kept = kept + lax.ppermute(cells, 'pulse', pairs).astype(jnp.float32)  9.13 us
    pallas_call x3, Pallas kernels, steer_part(): pl.pallas_call(functools.partial(steer_kernel, lines_total, tuple(group_h...  5.4 us
    unnamed x18, local copies, waits for them, and re-layouts  4.6 us
  transfers between devices with their start and end apart: 11, of which 5 were waited for; matrix products, arithmetic and copies ran while one was open for 0% of the time, Pallas kernels for 9%

profile of v4, /device:TPU:81, one launch (start us, length us, event | category | flops | bytes accessed | tf_op | source)
XLA Modules:
  0.0 107.5 jit_solution(14313355386538020469)
XLA Ops:
  0.0 0.9 fusion
  0.9 2.1 %collective-permute-start.1 = (bf16[2,8,2048]{2,1,0:T(8,128)(2,1)S(1)}, bf16[2,8,2048]{2,1,0:T(8,128)(2,1)S(1)}, u32[]{:S(2)}, u32[]{:S(2)}) collective-permute-start(bf16[2,8,2048]{2,1,0:T(8,128)(2,1)S(1)} %get-tuple-element.23), channel_id=1, source_target_pairs={{32,0},{64,32},{96,64},{33,1},{65,33},{97,65},{34,2},{66,34},{98,6... | collective-permute-start | bytes 196616 | tf_op jit(solution)/shard_map/ppermute | solution.py:335
  3.0 3.2 %collective-permute-start = (bf16[2,8,2048]{2,1,0:T(8,128)(2,1)S(1)}, bf16[2,8,2048]{2,1,0:T(8,128)(2,1)S(1)}, u32[]{:S(2)}, u32[]{:S(2)}) collective-permute-start(bf16[2,8,2048]{2,1,0:T(8,128)(2,1)S(1)} %get-tuple-element.24), channel_id=1, source_target_pairs={{0,32},{32,64},{64,96},{1,33},{33,65},{65,97},{2,34},{34,66},{66,9... | collective-permute-start | bytes 196616 | tf_op jit(solution)/shard_map/ppermute | solution.py:334
  6.2 0.0 copy-start
  6.2 0.9 copy-done
  7.1 0.7 copy-done.6
  7.9 2.7 %own_part.1 = (bf16[128,4224]{1,0:T(8,128)(2,1)S(1)}, bf16[128,4224]{1,0:T(8,128)(2,1)S(1)}, bf16[128,4224]{1,0:T(8,128)(2,1)S(1)}, f32[512,256]{1,0:T(8,128)S(1)}) custom-call(bf16[2,4096]{1,0:T(2,128)(2,1)S(1)} %copy-done.6, bf16[2,8,8192]{2,1,0:T(8,128)(2,1)S(1)} %copy-done), custom_call_target="tpu_custom_call" | custom-call | flops 2000000000 | bytes 8388608 | tf_op jit(solution)/shard_map/own_part/pallas_call | solution.py:123
  10.6 0.0 copy-start.5
  10.6 1.4 %edge_part.1.refs_0_ = bf16[528,256]{1,0:T(8,128)(2,1)S(1)} custom-call(s32[8]{0:T(128)S(1)} %copy-done.3, s32[8]{0:T(128)S(1)} %copy-done.4, bf16[2,8,2048]{2,1,0:T(8,128)(2,1)S(1)} %collective-permute-done.left_ref, bf16[2,8,2048]{2,1,0:T(8,128)(2,1)S(1)} %collective-permute-done.1.right_ref, bf16[128,4224]{1,0:T(8,128)(2,1)S(1)} %get-tuple-element.14.real_ref, ...), custom_call_target="tpu_custom_call" | custom-call | flops 300000000 | bytes 4194304 | tf_op jit(solution)/shard_map/edge_part/pallas_call | solution.py:176
  12.0 10.7 %collective-permute-start.4 = (bf16[528,256]{1,0:T(8,128)(2,1)S(1)}, bf16[528,256]{1,0:T(8,128)(2,1)S(1)}, u32[]{:S(2)}, u32[]{:S(2)}) collective-permute-start(bf16[528,256]{1,0:T(8,128)(2,1)S(1)} %edge_part.1.refs_0_), channel_id=1, source_target_pairs={{0,24},{1,25},{2,26},{3,27},{4,28},{5,29},{6,30},{7,31},{8,0},{9,1... | collective-permute-start | bytes 811016 | tf_op jit(solution)/shard_map/ppermute | solution.py:359
  22.6 1.9 %collective-permute-start.3 = (bf16[528,256]{1,0:T(8,128)(2,1)S(1)}, bf16[528,256]{1,0:T(8,128)(2,1)S(1)}, u32[]{:S(2)}, u32[]{:S(2)}) collective-permute-start(bf16[528,256]{1,0:T(8,128)(2,1)S(1)} %edge_part.1.refs_0_), channel_id=1, source_target_pairs={{0,8},{1,9},{2,10},{3,11},{4,12},{5,13},{6,14},{7,15},{8,16},{9,17... | collective-permute-start | bytes 811016 | tf_op jit(solution)/shard_map/ppermute | solution.py:358
  24.6 1.6 %steer_part.3 = bf16[8,16,1152]{2,1,0:T(8,128)(2,1)} custom-call(bf16[528,256]{1,0:T(8,128)(2,1)S(1)} %edge_part.1.refs_0_, bf16[8,256,128]{2,1,0:T(8,128)(2,1)S(1)} %copy-done.5), custom_call_target="tpu_custom_call" | custom-call | flops 20000000000 | bytes 1024 | tf_op jit(solution)/shard_map/steer_part/pallas_call | solution.py:248
  26.1 5.8 %all-to-all-start = ((bf16[8,16,1152]{2,1,0:T(8,128)(2,1)}), bf16[8,16,1152]{2,1,0:T(8,128)(2,1)S(1)}, u32[]{:S(2)}, u32[]{:S(2)}) async-start(bf16[8,16,1152]{2,1,0:T(8,128)(2,1)} %steer_part.3), calls=%async_computation | async-start | bytes 589824 | tf_op jit(solution)/shard_map/all_to_all | solution.py:352
  32.0 1.6 %steer_part.5 = bf16[8,16,1152]{2,1,0:T(8,128)(2,1)} custom-call(bf16[528,256]{1,0:T(8,128)(2,1)S(1)} %edge_part.1.refs_0_, bf16[8,256,128]{2,1,0:T(8,128)(2,1)S(1)} %copy-done.5), custom_call_target="tpu_custom_call" | custom-call | flops 20000000000 | bytes 1024 | tf_op jit(solution)/shard_map/steer_part/pallas_call | solution.py:248
  33.5 5.5 %all-to-all-done = bf16[8,16,1152]{2,1,0:T(8,128)(2,1)S(1)} async-done(((bf16[8,16,1152]{2,1,0:T(8,128)(2,1)}), bf16[8,16,1152]{2,1,0:T(8,128)(2,1)S(1)}, u32[]{:S(2)}, u32[]{:S(2)}) %all-to-all-start) | async-done | bytes 294944 | tf_op jit(solution)/shard_map/all_to_all | solution.py:352
  39.1 4.1 %all-to-all-start.2 = ((bf16[8,16,1152]{2,1,0:T(8,128)(2,1)}), bf16[8,16,1152]{2,1,0:T(8,128)(2,1)S(1)}, u32[]{:S(2)}, u32[]{:S(2)}) async-start(bf16[8,16,1152]{2,1,0:T(8,128)(2,1)} %steer_part.5), calls=%async_computation.2 | async-start | bytes 589824 | tf_op jit(solution)/shard_map/all_to_all | solution.py:352
  43.2 10.5 %collective-permute-start.2 = (bf16[8,16,1152]{2,1,0:T(8,128)(2,1)S(1)}, bf16[8,16,1152]{2,1,0:T(8,128)(2,1)S(1)}, u32[]{:S(2)}, u32[]{:S(2)}) collective-permute-start(bf16[8,16,1152]{2,1,0:T(8,128)(2,1)S(1)} %all-to-all-done), channel_id=1, source_target_pairs={{0,16},{1,17},{2,18},{3,19},{4,20},{5,21},{6,22},{7,23},{8,24},{9,... | collective-permute-start | bytes 884744 | tf_op jit(solution)/shard_map/ppermute | solution.py:361
  53.7 2.2 %steer_part.4 = bf16[8,32,1152]{2,1,0:T(8,128)(2,1)} custom-call(bf16[528,256]{1,0:T(8,128)(2,1)S(1)} %collective-permute-done.3.refs_0_, bf16[528,256]{1,0:T(8,128)(2,1)S(1)} %collective-permute-done.4.refs_1_, bf16[8,256,128]{2,1,0:T(8,128)(2,1)S(1)} %copy-done.5), custom_call_target="tpu_custom_call" | custom-call | flops 40000000000 | bytes 1024 | tf_op jit(solution)/shard_map/steer_part/pallas_call | solution.py:248
  56.0 5.1 %all-to-all-start.1 = ((bf16[8,32,1152]{2,1,0:T(8,128)(2,1)}), bf16[8,32,1152]{2,1,0:T(8,128)(2,1)S(1)}, u32[]{:S(2)}, u32[]{:S(2)}) async-start(bf16[8,32,1152]{2,1,0:T(8,128)(2,1)} %steer_part.4), calls=%async_computation.1 | async-start | bytes 1179648 | tf_op jit(solution)/shard_map/all_to_all | solution.py:352
  61.1 0.5 image_part.3.refs_1_
  61.6 1.3 %copy-done.7 = f32[4,128,1024]{2,1,0:T(8,128)} copy-done((f32[4,128,1024]{2,1,0:T(8,128)}, f32[4,128,1024]{2,1,0:T(8,128)S(1)}, u32[]{:S(2)}) %copy-start.7) | copy-done | bytes 2097176
  63.0 8.3 %all-to-all-done.1.refs_0_ = bf16[8,32,1152]{2,1,0:T(8,128)(2,1)S(1)} async-done(((bf16[8,32,1152]{2,1,0:T(8,128)(2,1)}), bf16[8,32,1152]{2,1,0:T(8,128)(2,1)S(1)}, u32[]{:S(2)}, u32[]{:S(2)}) %all-to-all-start.1) | async-done | bytes 589856 | tf_op jit(solution)/shard_map/all_to_all | solution.py:352
  71.3 1.6 %copy-done.8 = f32[4,128,1024]{2,1,0:T(8,128)S(1)} copy-done((f32[4,128,1024]{2,1,0:T(8,128)S(1)}, f32[4,128,1024]{2,1,0:T(8,128)}, u32[]{:S(2)}) %copy-start.8) | copy-done | bytes 2097176
  72.9 0.9 image_part.4.refs_1_
  73.7 4.6 %collective-permute-done.2.refs_0_ = bf16[8,16,1152]{2,1,0:T(8,128)(2,1)S(1)} collective-permute-done((bf16[8,16,1152]{2,1,0:T(8,128)(2,1)S(1)}, bf16[8,16,1152]{2,1,0:T(8,128)(2,1)S(1)}, u32[]{:S(2)}, u32[]{:S(2)}) %collective-permute-start.2) | collective-permute-done | bytes 294944 | tf_op jit(solution)/shard_map/ppermute | solution.py:361
  78.3 0.6 image_part.5
  78.9 1.9 %collective-permute-start.5 = (bf16[128,1024]{1,0:T(8,128)(2,1)S(1)}, bf16[128,1024]{1,0:T(8,128)(2,1)S(1)}, u32[]{:S(2)}, u32[]{:S(2)}) collective-permute-start(bf16[128,1024]{1,0:T(8,128)(2,1)S(1)} %get-tuple-element.20), channel_id=1, source_target_pairs={{0,256},{128,384},{256,0},{384,128},{1,257},{129,385},{257,1},{385... | collective-permute-start | bytes 786440 | tf_op jit(solution)/shard_map/ppermute | solution.py:373
  80.8 5.3 %collective-permute-start.6 = (bf16[128,1024]{1,0:T(8,128)(2,1)S(1)}, bf16[128,1024]{1,0:T(8,128)(2,1)S(1)}, u32[]{:S(2)}, u32[]{:S(2)}) collective-permute-start(bf16[128,1024]{1,0:T(8,128)(2,1)S(1)} %get-tuple-element.21), channel_id=1, source_target_pairs={{0,128},{128,256},{256,384},{384,0},{1,129},{129,257},{257,385},{3... | collective-permute-start | bytes 786440 | tf_op jit(solution)/shard_map/ppermute | solution.py:373
  86.1 1.9 %collective-permute-start.7 = (bf16[128,1024]{1,0:T(8,128)(2,1)S(1)}, bf16[128,1024]{1,0:T(8,128)(2,1)S(1)}, u32[]{:S(2)}, u32[]{:S(2)}) collective-permute-start(bf16[128,1024]{1,0:T(8,128)(2,1)S(1)} %get-tuple-element.22), channel_id=1, source_target_pairs={{0,384},{128,0},{256,128},{384,256},{1,385},{129,1},{257,129},{385... | collective-permute-start | bytes 786440 | tf_op jit(solution)/shard_map/ppermute | solution.py:373
  88.1 7.9 %collective-permute-done.5 = bf16[128,1024]{1,0:T(8,128)(2,1)S(1)} collective-permute-done((bf16[128,1024]{1,0:T(8,128)(2,1)S(1)}, bf16[128,1024]{1,0:T(8,128)(2,1)S(1)}, u32[]{:S(2)}, u32[]{:S(2)}) %collective-permute-start.5) | collective-permute-done | bytes 262176 | tf_op jit(solution)/shard_map/ppermute | solution.py:373
  96.0 10.5 %collective-permute-done.6 = bf16[128,1024]{1,0:T(8,128)(2,1)S(1)} collective-permute-done((bf16[128,1024]{1,0:T(8,128)(2,1)S(1)}, bf16[128,1024]{1,0:T(8,128)(2,1)S(1)}, u32[]{:S(2)}, u32[]{:S(2)}) %collective-permute-start.6) | collective-permute-done | bytes 262176 | tf_op jit(solution)/shard_map/ppermute | solution.py:373
  106.5 0.9 convert_add_fusion
  (18 shorter events, 0.0 us)
Async XLA Ops:
  0.9 9.6 %collective-permute-start.1 = (bf16[2,8,2048]{2,1,0:T(8,128)(2,1)S(1)}, bf16[2,8,2048]{2,1,0:T(8,128)(2,1)S(1)}, u32[]{:S(2)}, u32[]{:S(2)}) collective-permute-start(bf16[2,8,2048]{2,1,0:T(8,128)(2,1)S(1)} %get-tuple-element.23), channel_id=1, source_target_pairs={{32,0},{64,32},{96,64},{33,1},{65,33},{97,65},{34,2},{66,34},{98,6... | collective-permute-start | bytes 196616 | tf_op jit(solution)/shard_map/ppermute | solution.py:335
  3.0 7.6 %collective-permute-start = (bf16[2,8,2048]{2,1,0:T(8,128)(2,1)S(1)}, bf16[2,8,2048]{2,1,0:T(8,128)(2,1)S(1)}, u32[]{:S(2)}, u32[]{:S(2)}) collective-permute-start(bf16[2,8,2048]{2,1,0:T(8,128)(2,1)S(1)} %get-tuple-element.24), channel_id=1, source_target_pairs={{0,32},{32,64},{64,96},{1,33},{33,65},{65,97},{2,34},{34,66},{66,9... | collective-permute-start | bytes 196616 | tf_op jit(solution)/shard_map/ppermute | solution.py:334
  6.2 1.0 copy-start
  7.1 0.7 copy-start.6
  7.9 2.7 %copy-start.1 = (s32[8,32,1]{1,2,0:T(1,128)S(1)}, s32[8,32,1]{1,2,0:T(1,128)}, u32[]{:S(2)}) copy-start(s32[8,32,1]{1,2,0:T(1,128)} %param.10) | copy-start | bytes 3076
  7.9 2.7 %copy-start.2 = (s32[8,32]{1,0:T(8,128)S(1)}, s32[8,32]{1,0:T(8,128)}, u32[]{:S(2)}) copy-start(s32[8,32]{1,0:T(8,128)} %visible_ref.1) | copy-start | bytes 3076
  7.9 2.7 %copy-start.3 = (s32[8]{0:T(128)S(1)}, s32[8]{0:T(128)}, u32[]{:S(2)}) copy-start(s32[8]{0:T(128)} %step_ref.1) | copy-start | bytes 100
  7.9 2.7 %copy-start.4 = (s32[8]{0:T(128)S(1)}, s32[8]{0:T(128)}, u32[]{:S(2)}) copy-start(s32[8]{0:T(128)} %bin_ref.1) | copy-start | bytes 100
  10.6 14.0 %copy-start.5 = (bf16[8,256,128]{2,1,0:T(8,128)(2,1)S(1)}, bf16[8,256,128]{2,1,0:T(8,128)(2,1)}, u32[]{:S(2)}) copy-start(bf16[8,256,128]{2,1,0:T(8,128)(2,1)} %refs_1_.3) | copy-start | bytes 1572868
  12.0 41.8 %collective-permute-start.4 = (bf16[528,256]{1,0:T(8,128)(2,1)S(1)}, bf16[528,256]{1,0:T(8,128)(2,1)S(1)}, u32[]{:S(2)}, u32[]{:S(2)}) collective-permute-start(bf16[528,256]{1,0:T(8,128)(2,1)S(1)} %edge_part.1.refs_0_), channel_id=1, source_target_pairs={{0,24},{1,25},{2,26},{3,27},{4,28},{5,29},{6,30},{7,31},{8,0},{9,1... | collective-permute-start | bytes 811016 | tf_op jit(solution)/shard_map/ppermute | solution.py:359
  22.6 31.1 %collective-permute-start.3 = (bf16[528,256]{1,0:T(8,128)(2,1)S(1)}, bf16[528,256]{1,0:T(8,128)(2,1)S(1)}, u32[]{:S(2)}, u32[]{:S(2)}) collective-permute-start(bf16[528,256]{1,0:T(8,128)(2,1)S(1)} %edge_part.1.refs_0_), channel_id=1, source_target_pairs={{0,8},{1,9},{2,10},{3,11},{4,12},{5,13},{6,14},{7,15},{8,16},{9,17... | collective-permute-start | bytes 811016 | tf_op jit(solution)/shard_map/ppermute | solution.py:358
  26.1 12.9 %all-to-all-start = ((bf16[8,16,1152]{2,1,0:T(8,128)(2,1)}), bf16[8,16,1152]{2,1,0:T(8,128)(2,1)S(1)}, u32[]{:S(2)}, u32[]{:S(2)}) async-start(bf16[8,16,1152]{2,1,0:T(8,128)(2,1)} %steer_part.3), calls=%async_computation | async-start | bytes 589824 | tf_op jit(solution)/shard_map/all_to_all | solution.py:352
  39.1 16.9 %all-to-all-start.2 = ((bf16[8,16,1152]{2,1,0:T(8,128)(2,1)}), bf16[8,16,1152]{2,1,0:T(8,128)(2,1)S(1)}, u32[]{:S(2)}, u32[]{:S(2)}) async-start(bf16[8,16,1152]{2,1,0:T(8,128)(2,1)} %steer_part.5), calls=%async_computation.2 | async-start | bytes 589824 | tf_op jit(solution)/shard_map/all_to_all | solution.py:352
  43.2 35.2 %collective-permute-start.2 = (bf16[8,16,1152]{2,1,0:T(8,128)(2,1)S(1)}, bf16[8,16,1152]{2,1,0:T(8,128)(2,1)S(1)}, u32[]{:S(2)}, u32[]{:S(2)}) collective-permute-start(bf16[8,16,1152]{2,1,0:T(8,128)(2,1)S(1)} %all-to-all-done), channel_id=1, source_target_pairs={{0,16},{1,17},{2,18},{3,19},{4,20},{5,21},{6,22},{7,23},{8,24},{9,... | collective-permute-start | bytes 884744 | tf_op jit(solution)/shard_map/ppermute | solution.py:361
  56.0 15.3 %all-to-all-start.1 = ((bf16[8,32,1152]{2,1,0:T(8,128)(2,1)}), bf16[8,32,1152]{2,1,0:T(8,128)(2,1)S(1)}, u32[]{:S(2)}, u32[]{:S(2)}) async-start(bf16[8,32,1152]{2,1,0:T(8,128)(2,1)} %steer_part.4), calls=%async_computation.1 | async-start | bytes 1179648 | tf_op jit(solution)/shard_map/all_to_all | solution.py:352
  61.6 1.3 %copy-start.7 = (f32[4,128,1024]{2,1,0:T(8,128)}, f32[4,128,1024]{2,1,0:T(8,128)S(1)}, u32[]{:S(2)}) copy-start(f32[4,128,1024]{2,1,0:T(8,128)S(1)} %image_part.3.refs_1_) | copy-start | bytes 6291460
  71.3 1.6 %copy-start.8 = (f32[4,128,1024]{2,1,0:T(8,128)S(1)}, f32[4,128,1024]{2,1,0:T(8,128)}, u32[]{:S(2)}) copy-start(f32[4,128,1024]{2,1,0:T(8,128)} %copy-done.7) | copy-start | bytes 6291460
  78.9 17.1 %collective-permute-start.5 = (bf16[128,1024]{1,0:T(8,128)(2,1)S(1)}, bf16[128,1024]{1,0:T(8,128)(2,1)S(1)}, u32[]{:S(2)}, u32[]{:S(2)}) collective-permute-start(bf16[128,1024]{1,0:T(8,128)(2,1)S(1)} %get-tuple-element.20), channel_id=1, source_target_pairs={{0,256},{128,384},{256,0},{384,128},{1,257},{129,385},{257,1},{385... | collective-permute-start | bytes 786440 | tf_op jit(solution)/shard_map/ppermute | solution.py:373
  80.8 25.7 %collective-permute-start.6 = (bf16[128,1024]{1,0:T(8,128)(2,1)S(1)}, bf16[128,1024]{1,0:T(8,128)(2,1)S(1)}, u32[]{:S(2)}, u32[]{:S(2)}) collective-permute-start(bf16[128,1024]{1,0:T(8,128)(2,1)S(1)} %get-tuple-element.21), channel_id=1, source_target_pairs={{0,128},{128,256},{256,384},{384,0},{1,129},{129,257},{257,385},{3... | collective-permute-start | bytes 786440 | tf_op jit(solution)/shard_map/ppermute | solution.py:373
  86.1 20.4 %collective-permute-start.7 = (bf16[128,1024]{1,0:T(8,128)(2,1)S(1)}, bf16[128,1024]{1,0:T(8,128)(2,1)S(1)}, u32[]{:S(2)}, u32[]{:S(2)}) collective-permute-start(bf16[128,1024]{1,0:T(8,128)(2,1)S(1)} %get-tuple-element.22), channel_id=1, source_target_pairs={{0,384},{128,0},{256,128},{384,256},{1,385},{129,1},{257,129},{385... | collective-permute-start | bytes 786440 | tf_op jit(solution)/shard_map/ppermute | solution.py:373

commit v5 on v3

--- a/solution.py
+++ b/solution.py
@@ -20,7 +20,7 @@
 IMAGE_COST = 20000000000
 STEER_COST = 20000000000
 
-SINE = tuple((-1.0) ** n * (2.0 * math.pi) ** (2 * n + 1) / math.factorial(2 * n + 1) for n in range(8))
+SINE = tuple((-1.0) ** n * (2.0 * math.pi) ** (2 * n + 1) / math.factorial(2 * n + 1) for n in range(7))
 
 
 def cosine_of_turns(turns, total):

time: 108 us -> 108 us (level)
  no operation moved by 1% of the time
where the time goes in v5:
time: 108 us; the launch traced here: 107 us
  starting transfers between devices  52.6 us (49%)
  waiting for transfers between devices  37 us (34%)
  Pallas kernels  11.3 us (10%)
  local copies, waits for them, and re-layouts  5.48 us (5%)
    ppermute x3, waiting for transfers between devices, local(): kept = kept + lax.ppermute(cells, 'pulse', pairs).astype(jnp.float32)  18.5 us
    all_to_all x3, starting transfers between devices, exchange(): lax.all_to_all(steered, 'tile', 0, 0, axis_index_groups=groups, tiled=True)  15 us
    all_to_all x3, waiting for transfers between devices, exchange(): lax.all_to_all(steered, 'tile', 0, 0, axis_index_groups=groups, tiled=True)  13.8 us
    ppermute x1, starting transfers between devices, local(): above = lax.ppermute(mine, 'tile', group_shift(-1))  10.7 us
    ppermute x1, starting transfers between devices, local(): opposite = lax.ppermute(exchange(steered), 'tile', group_shift(far // 2))  10.5 us
    ppermute x3, starting transfers between devices, local(): kept = kept + lax.ppermute(cells, 'pulse', pairs).astype(jnp.float32)  9.14 us
    pallas_call x3, Pallas kernels, steer_part(): pl.pallas_call(functools.partial(steer_kernel, lines_total, tuple(group_h...  5.4 us
    ppermute x1, waiting for transfers between devices, local(): opposite = lax.ppermute(exchange(steered), 'tile', group_shift(far // 2))  4.61 us
  transfers between devices with their start and end apart: 11, of which 6 were waited for; matrix products, arithmetic and copies ran while one was open for 0% of the time, Pallas kernels for 9%

profile of v5, /device:TPU:81, one launch (start us, length us, event | category | flops | bytes accessed | tf_op | source)
XLA Modules:
  0.0 107.5 jit_solution(3835588403652117750)
XLA Ops:
  0.0 0.9 fusion
  0.9 2.1 %collective-permute-start.1 = (bf16[2,8,2048]{2,1,0:T(8,128)(2,1)S(1)}, bf16[2,8,2048]{2,1,0:T(8,128)(2,1)S(1)}, u32[]{:S(2)}, u32[]{:S(2)}) collective-permute-start(bf16[2,8,2048]{2,1,0:T(8,128)(2,1)S(1)} %get-tuple-element.23), channel_id=1, source_target_pairs={{32,0},{64,32},{96,64},{33,1},{65,33},{97,65},{34,2},{66,34},{98,6... | collective-permute-start | bytes 196616 | tf_op jit(solution)/shard_map/ppermute | solution.py:335
  3.0 3.2 %collective-permute-start = (bf16[2,8,2048]{2,1,0:T(8,128)(2,1)S(1)}, bf16[2,8,2048]{2,1,0:T(8,128)(2,1)S(1)}, u32[]{:S(2)}, u32[]{:S(2)}) collective-permute-start(bf16[2,8,2048]{2,1,0:T(8,128)(2,1)S(1)} %get-tuple-element.24), channel_id=1, source_target_pairs={{0,32},{32,64},{64,96},{1,33},{33,65},{65,97},{2,34},{34,66},{66,9... | collective-permute-start | bytes 196616 | tf_op jit(solution)/shard_map/ppermute | solution.py:334
  6.2 0.9 copy-done
  7.1 0.7 copy-done.6
  7.9 2.7 %own_part.1 = (bf16[128,4224]{1,0:T(8,128)(2,1)S(1)}, bf16[128,4224]{1,0:T(8,128)(2,1)S(1)}, bf16[128,4224]{1,0:T(8,128)(2,1)S(1)}, f32[512,256]{1,0:T(8,128)S(1)}) custom-call(bf16[2,4096]{1,0:T(2,128)(2,1)S(1)} %copy-done.6, bf16[2,8,8192]{2,1,0:T(8,128)(2,1)S(1)} %copy-done), custom_call_target="tpu_custom_call" | custom-call | flops 2000000000 | bytes 8388608 | tf_op jit(solution)/shard_map/own_part/pallas_call | solution.py:123
  10.6 0.0 copy-start.5
  10.6 1.4 %edge_part.1.refs_0_ = bf16[528,256]{1,0:T(8,128)(2,1)S(1)} custom-call(s32[8]{0:T(128)S(1)} %copy-done.3, s32[8]{0:T(128)S(1)} %copy-done.4, bf16[2,8,2048]{2,1,0:T(8,128)(2,1)S(1)} %collective-permute-done.left_ref, bf16[2,8,2048]{2,1,0:T(8,128)(2,1)S(1)} %collective-permute-done.1.right_ref, bf16[128,4224]{1,0:T(8,128)(2,1)S(1)} %get-tuple-element.14.real_ref, ...), custom_call_target="tpu_custom_call" | custom-call | flops 300000000 | bytes 4194304 | tf_op jit(solution)/shard_map/edge_part/pallas_call | solution.py:176
  12.0 10.7 %collective-permute-start.4 = (bf16[528,256]{1,0:T(8,128)(2,1)S(1)}, bf16[528,256]{1,0:T(8,128)(2,1)S(1)}, u32[]{:S(2)}, u32[]{:S(2)}) collective-permute-start(bf16[528,256]{1,0:T(8,128)(2,1)S(1)} %edge_part.1.refs_0_), channel_id=1, source_target_pairs={{0,24},{1,25},{2,26},{3,27},{4,28},{5,29},{6,30},{7,31},{8,0},{9,1... | collective-permute-start | bytes 811016 | tf_op jit(solution)/shard_map/ppermute | solution.py:359
  22.6 1.9 %collective-permute-start.3 = (bf16[528,256]{1,0:T(8,128)(2,1)S(1)}, bf16[528,256]{1,0:T(8,128)(2,1)S(1)}, u32[]{:S(2)}, u32[]{:S(2)}) collective-permute-start(bf16[528,256]{1,0:T(8,128)(2,1)S(1)} %edge_part.1.refs_0_), channel_id=1, source_target_pairs={{0,8},{1,9},{2,10},{3,11},{4,12},{5,13},{6,14},{7,15},{8,16},{9,17... | collective-permute-start | bytes 811016 | tf_op jit(solution)/shard_map/ppermute | solution.py:358
  24.6 1.6 %steer_part.3 = bf16[8,16,1152]{2,1,0:T(8,128)(2,1)} custom-call(bf16[528,256]{1,0:T(8,128)(2,1)S(1)} %edge_part.1.refs_0_, bf16[8,256,128]{2,1,0:T(8,128)(2,1)S(1)} %copy-done.5), custom_call_target="tpu_custom_call" | custom-call | flops 20000000000 | bytes 1024 | tf_op jit(solution)/shard_map/steer_part/pallas_call | solution.py:248
  26.1 5.8 %all-to-all-start = ((bf16[8,16,1152]{2,1,0:T(8,128)(2,1)}), bf16[8,16,1152]{2,1,0:T(8,128)(2,1)S(1)}, u32[]{:S(2)}, u32[]{:S(2)}) async-start(bf16[8,16,1152]{2,1,0:T(8,128)(2,1)} %steer_part.3), calls=%async_computation | async-start | bytes 589824 | tf_op jit(solution)/shard_map/all_to_all | solution.py:352
  31.9 1.6 %steer_part.5 = bf16[8,16,1152]{2,1,0:T(8,128)(2,1)} custom-call(bf16[528,256]{1,0:T(8,128)(2,1)S(1)} %edge_part.1.refs_0_, bf16[8,256,128]{2,1,0:T(8,128)(2,1)S(1)} %copy-done.5), custom_call_target="tpu_custom_call" | custom-call | flops 20000000000 | bytes 1024 | tf_op jit(solution)/shard_map/steer_part/pallas_call | solution.py:248
  33.5 5.5 %all-to-all-done = bf16[8,16,1152]{2,1,0:T(8,128)(2,1)S(1)} async-done(((bf16[8,16,1152]{2,1,0:T(8,128)(2,1)}), bf16[8,16,1152]{2,1,0:T(8,128)(2,1)S(1)}, u32[]{:S(2)}, u32[]{:S(2)}) %all-to-all-start) | async-done | bytes 294944 | tf_op jit(solution)/shard_map/all_to_all | solution.py:352
  39.1 4.1 %all-to-all-start.2 = ((bf16[8,16,1152]{2,1,0:T(8,128)(2,1)}), bf16[8,16,1152]{2,1,0:T(8,128)(2,1)S(1)}, u32[]{:S(2)}, u32[]{:S(2)}) async-start(bf16[8,16,1152]{2,1,0:T(8,128)(2,1)} %steer_part.5), calls=%async_computation.2 | async-start | bytes 589824 | tf_op jit(solution)/shard_map/all_to_all | solution.py:352
  43.2 10.5 %collective-permute-start.2 = (bf16[8,16,1152]{2,1,0:T(8,128)(2,1)S(1)}, bf16[8,16,1152]{2,1,0:T(8,128)(2,1)S(1)}, u32[]{:S(2)}, u32[]{:S(2)}) collective-permute-start(bf16[8,16,1152]{2,1,0:T(8,128)(2,1)S(1)} %all-to-all-done), channel_id=1, source_target_pairs={{0,16},{1,17},{2,18},{3,19},{4,20},{5,21},{6,22},{7,23},{8,24},{9,... | collective-permute-start | bytes 884744 | tf_op jit(solution)/shard_map/ppermute | solution.py:361
  53.7 2.3 %steer_part.4 = bf16[8,32,1152]{2,1,0:T(8,128)(2,1)} custom-call(bf16[528,256]{1,0:T(8,128)(2,1)S(1)} %collective-permute-done.3.refs_0_, bf16[528,256]{1,0:T(8,128)(2,1)S(1)} %collective-permute-done.4.refs_1_, bf16[8,256,128]{2,1,0:T(8,128)(2,1)S(1)} %copy-done.5), custom_call_target="tpu_custom_call" | custom-call | flops 40000000000 | bytes 1024 | tf_op jit(solution)/shard_map/steer_part/pallas_call | solution.py:248
  56.0 5.1 %all-to-all-start.1 = ((bf16[8,32,1152]{2,1,0:T(8,128)(2,1)}), bf16[8,32,1152]{2,1,0:T(8,128)(2,1)S(1)}, u32[]{:S(2)}, u32[]{:S(2)}) async-start(bf16[8,32,1152]{2,1,0:T(8,128)(2,1)} %steer_part.4), calls=%async_computation.1 | async-start | bytes 1179648 | tf_op jit(solution)/shard_map/all_to_all | solution.py:352
  61.1 0.5 image_part.3.refs_1_
  61.6 1.3 %copy-done.7 = f32[4,128,1024]{2,1,0:T(8,128)} copy-done((f32[4,128,1024]{2,1,0:T(8,128)}, f32[4,128,1024]{2,1,0:T(8,128)S(1)}, u32[]{:S(2)}) %copy-start.7) | copy-done | bytes 2097176
  63.0 8.3 %all-to-all-done.1.refs_0_ = bf16[8,32,1152]{2,1,0:T(8,128)(2,1)S(1)} async-done(((bf16[8,32,1152]{2,1,0:T(8,128)(2,1)}), bf16[8,32,1152]{2,1,0:T(8,128)(2,1)S(1)}, u32[]{:S(2)}, u32[]{:S(2)}) %all-to-all-start.1) | async-done | bytes 589856 | tf_op jit(solution)/shard_map/all_to_all | solution.py:352
  71.3 1.6 %copy-done.8 = f32[4,128,1024]{2,1,0:T(8,128)S(1)} copy-done((f32[4,128,1024]{2,1,0:T(8,128)S(1)}, f32[4,128,1024]{2,1,0:T(8,128)}, u32[]{:S(2)}) %copy-start.8) | copy-done | bytes 2097176
  72.9 0.9 image_part.4.refs_1_
  73.7 4.6 %collective-permute-done.2.refs_0_ = bf16[8,16,1152]{2,1,0:T(8,128)(2,1)S(1)} collective-permute-done((bf16[8,16,1152]{2,1,0:T(8,128)(2,1)S(1)}, bf16[8,16,1152]{2,1,0:T(8,128)(2,1)S(1)}, u32[]{:S(2)}, u32[]{:S(2)}) %collective-permute-start.2) | collective-permute-done | bytes 294944 | tf_op jit(solution)/shard_map/ppermute | solution.py:361
  78.3 0.5 image_part.5
  78.9 1.9 %collective-permute-start.5 = (bf16[128,1024]{1,0:T(8,128)(2,1)S(1)}, bf16[128,1024]{1,0:T(8,128)(2,1)S(1)}, u32[]{:S(2)}, u32[]{:S(2)}) collective-permute-start(bf16[128,1024]{1,0:T(8,128)(2,1)S(1)} %get-tuple-element.20), channel_id=1, source_target_pairs={{0,256},{128,384},{256,0},{384,128},{1,257},{129,385},{257,1},{385... | collective-permute-start | bytes 786440 | tf_op jit(solution)/shard_map/ppermute | solution.py:373
  80.8 4.1 %collective-permute-start.6 = (bf16[128,1024]{1,0:T(8,128)(2,1)S(1)}, bf16[128,1024]{1,0:T(8,128)(2,1)S(1)}, u32[]{:S(2)}, u32[]{:S(2)}) collective-permute-start(bf16[128,1024]{1,0:T(8,128)(2,1)S(1)} %get-tuple-element.21), channel_id=1, source_target_pairs={{0,384},{128,0},{256,128},{384,256},{1,385},{129,1},{257,129},{385... | collective-permute-start | bytes 786440 | tf_op jit(solution)/shard_map/ppermute | solution.py:373
  84.9 3.1 %collective-permute-start.7 = (bf16[128,1024]{1,0:T(8,128)(2,1)S(1)}, bf16[128,1024]{1,0:T(8,128)(2,1)S(1)}, u32[]{:S(2)}, u32[]{:S(2)}) collective-permute-start(bf16[128,1024]{1,0:T(8,128)(2,1)S(1)} %get-tuple-element.22), channel_id=1, source_target_pairs={{0,128},{128,256},{256,384},{384,0},{1,129},{129,257},{257,385},{3... | collective-permute-start | bytes 786440 | tf_op jit(solution)/shard_map/ppermute | solution.py:373
  88.0 2.2 %collective-permute-done.5 = bf16[128,1024]{1,0:T(8,128)(2,1)S(1)} collective-permute-done((bf16[128,1024]{1,0:T(8,128)(2,1)S(1)}, bf16[128,1024]{1,0:T(8,128)(2,1)S(1)}, u32[]{:S(2)}, u32[]{:S(2)}) %collective-permute-start.5) | collective-permute-done | bytes 262176 | tf_op jit(solution)/shard_map/ppermute | solution.py:373
  90.3 12.8 %collective-permute-done.6 = bf16[128,1024]{1,0:T(8,128)(2,1)S(1)} collective-permute-done((bf16[128,1024]{1,0:T(8,128)(2,1)S(1)}, bf16[128,1024]{1,0:T(8,128)(2,1)S(1)}, u32[]{:S(2)}, u32[]{:S(2)}) %collective-permute-start.6) | collective-permute-done | bytes 262176 | tf_op jit(solution)/shard_map/ppermute | solution.py:373
  103.1 3.4 %collective-permute-done.7 = bf16[128,1024]{1,0:T(8,128)(2,1)S(1)} collective-permute-done((bf16[128,1024]{1,0:T(8,128)(2,1)S(1)}, bf16[128,1024]{1,0:T(8,128)(2,1)S(1)}, u32[]{:S(2)}, u32[]{:S(2)}) %collective-permute-start.7) | collective-permute-done | bytes 262176 | tf_op jit(solution)/shard_map/ppermute | solution.py:373
  106.5 0.9 convert_add_fusion
  (18 shorter events, 0.0 us)
Async XLA Ops:
  0.9 9.6 %collective-permute-start.1 = (bf16[2,8,2048]{2,1,0:T(8,128)(2,1)S(1)}, bf16[2,8,2048]{2,1,0:T(8,128)(2,1)S(1)}, u32[]{:S(2)}, u32[]{:S(2)}) collective-permute-start(bf16[2,8,2048]{2,1,0:T(8,128)(2,1)S(1)} %get-tuple-element.23), channel_id=1, source_target_pairs={{32,0},{64,32},{96,64},{33,1},{65,33},{97,65},{34,2},{66,34},{98,6... | collective-permute-start | bytes 196616 | tf_op jit(solution)/shard_map/ppermute | solution.py:335
  3.0 7.6 %collective-permute-start = (bf16[2,8,2048]{2,1,0:T(8,128)(2,1)S(1)}, bf16[2,8,2048]{2,1,0:T(8,128)(2,1)S(1)}, u32[]{:S(2)}, u32[]{:S(2)}) collective-permute-start(bf16[2,8,2048]{2,1,0:T(8,128)(2,1)S(1)} %get-tuple-element.24), channel_id=1, source_target_pairs={{0,32},{32,64},{64,96},{1,33},{33,65},{65,97},{2,34},{34,66},{66,9... | collective-permute-start | bytes 196616 | tf_op jit(solution)/shard_map/ppermute | solution.py:334
  6.2 1.0 copy-start
  7.1 0.7 copy-start.6
  7.9 2.7 %copy-start.1 = (s32[8,32,1]{1,2,0:T(1,128)S(1)}, s32[8,32,1]{1,2,0:T(1,128)}, u32[]{:S(2)}) copy-start(s32[8,32,1]{1,2,0:T(1,128)} %param.10) | copy-start | bytes 3076
  7.9 2.7 %copy-start.2 = (s32[8,32]{1,0:T(8,128)S(1)}, s32[8,32]{1,0:T(8,128)}, u32[]{:S(2)}) copy-start(s32[8,32]{1,0:T(8,128)} %visible_ref.1) | copy-start | bytes 3076
  7.9 2.7 %copy-start.3 = (s32[8]{0:T(128)S(1)}, s32[8]{0:T(128)}, u32[]{:S(2)}) copy-start(s32[8]{0:T(128)} %step_ref.1) | copy-start | bytes 100
  7.9 2.7 %copy-start.4 = (s32[8]{0:T(128)S(1)}, s32[8]{0:T(128)}, u32[]{:S(2)}) copy-start(s32[8]{0:T(128)} %bin_ref.1) | copy-start | bytes 100
  10.6 14.0 %copy-start.5 = (bf16[8,256,128]{2,1,0:T(8,128)(2,1)S(1)}, bf16[8,256,128]{2,1,0:T(8,128)(2,1)}, u32[]{:S(2)}) copy-start(bf16[8,256,128]{2,1,0:T(8,128)(2,1)} %refs_1_.3) | copy-start | bytes 1572868
  12.0 41.8 %collective-permute-start.4 = (bf16[528,256]{1,0:T(8,128)(2,1)S(1)}, bf16[528,256]{1,0:T(8,128)(2,1)S(1)}, u32[]{:S(2)}, u32[]{:S(2)}) collective-permute-start(bf16[528,256]{1,0:T(8,128)(2,1)S(1)} %edge_part.1.refs_0_), channel_id=1, source_target_pairs={{0,24},{1,25},{2,26},{3,27},{4,28},{5,29},{6,30},{7,31},{8,0},{9,1... | collective-permute-start | bytes 811016 | tf_op jit(solution)/shard_map/ppermute | solution.py:359
  22.6 31.1 %collective-permute-start.3 = (bf16[528,256]{1,0:T(8,128)(2,1)S(1)}, bf16[528,256]{1,0:T(8,128)(2,1)S(1)}, u32[]{:S(2)}, u32[]{:S(2)}) collective-permute-start(bf16[528,256]{1,0:T(8,128)(2,1)S(1)} %edge_part.1.refs_0_), channel_id=1, source_target_pairs={{0,8},{1,9},{2,10},{3,11},{4,12},{5,13},{6,14},{7,15},{8,16},{9,17... | collective-permute-start | bytes 811016 | tf_op jit(solution)/shard_map/ppermute | solution.py:358
  26.1 12.9 %all-to-all-start = ((bf16[8,16,1152]{2,1,0:T(8,128)(2,1)}), bf16[8,16,1152]{2,1,0:T(8,128)(2,1)S(1)}, u32[]{:S(2)}, u32[]{:S(2)}) async-start(bf16[8,16,1152]{2,1,0:T(8,128)(2,1)} %steer_part.3), calls=%async_computation | async-start | bytes 589824 | tf_op jit(solution)/shard_map/all_to_all | solution.py:352
  39.1 16.9 %all-to-all-start.2 = ((bf16[8,16,1152]{2,1,0:T(8,128)(2,1)}), bf16[8,16,1152]{2,1,0:T(8,128)(2,1)S(1)}, u32[]{:S(2)}, u32[]{:S(2)}) async-start(bf16[8,16,1152]{2,1,0:T(8,128)(2,1)} %steer_part.5), calls=%async_computation.2 | async-start | bytes 589824 | tf_op jit(solution)/shard_map/all_to_all | solution.py:352
  43.2 35.2 %collective-permute-start.2 = (bf16[8,16,1152]{2,1,0:T(8,128)(2,1)S(1)}, bf16[8,16,1152]{2,1,0:T(8,128)(2,1)S(1)}, u32[]{:S(2)}, u32[]{:S(2)}) collective-permute-start(bf16[8,16,1152]{2,1,0:T(8,128)(2,1)S(1)} %all-to-all-done), channel_id=1, source_target_pairs={{0,16},{1,17},{2,18},{3,19},{4,20},{5,21},{6,22},{7,23},{8,24},{9,... | collective-permute-start | bytes 884744 | tf_op jit(solution)/shard_map/ppermute | solution.py:361
  56.0 15.3 %all-to-all-start.1 = ((bf16[8,32,1152]{2,1,0:T(8,128)(2,1)}), bf16[8,32,1152]{2,1,0:T(8,128)(2,1)S(1)}, u32[]{:S(2)}, u32[]{:S(2)}) async-start(bf16[8,32,1152]{2,1,0:T(8,128)(2,1)} %steer_part.4), calls=%async_computation.1 | async-start | bytes 1179648 | tf_op jit(solution)/shard_map/all_to_all | solution.py:352
  61.6 1.3 %copy-start.7 = (f32[4,128,1024]{2,1,0:T(8,128)}, f32[4,128,1024]{2,1,0:T(8,128)S(1)}, u32[]{:S(2)}) copy-start(f32[4,128,1024]{2,1,0:T(8,128)S(1)} %image_part.3.refs_1_) | copy-start | bytes 6291460
  71.3 1.6 %copy-start.8 = (f32[4,128,1024]{2,1,0:T(8,128)S(1)}, f32[4,128,1024]{2,1,0:T(8,128)}, u32[]{:S(2)}) copy-start(f32[4,128,1024]{2,1,0:T(8,128)} %copy-done.7) | copy-start | bytes 6291460
  78.9 11.4 %collective-permute-start.5 = (bf16[128,1024]{1,0:T(8,128)(2,1)S(1)}, bf16[128,1024]{1,0:T(8,128)(2,1)S(1)}, u32[]{:S(2)}, u32[]{:S(2)}) collective-permute-start(bf16[128,1024]{1,0:T(8,128)(2,1)S(1)} %get-tuple-element.20), channel_id=1, source_target_pairs={{0,256},{128,384},{256,0},{384,128},{1,257},{129,385},{257,1},{385... | collective-permute-start | bytes 786440 | tf_op jit(solution)/shard_map/ppermute | solution.py:373
  80.8 22.3 %collective-permute-start.6 = (bf16[128,1024]{1,0:T(8,128)(2,1)S(1)}, bf16[128,1024]{1,0:T(8,128)(2,1)S(1)}, u32[]{:S(2)}, u32[]{:S(2)}) collective-permute-start(bf16[128,1024]{1,0:T(8,128)(2,1)S(1)} %get-tuple-element.21), channel_id=1, source_target_pairs={{0,384},{128,0},{256,128},{384,256},{1,385},{129,1},{257,129},{385... | collective-permute-start | bytes 786440 | tf_op jit(solution)/shard_map/ppermute | solution.py:373
  84.9 21.6 %collective-permute-start.7 = (bf16[128,1024]{1,0:T(8,128)(2,1)S(1)}, bf16[128,1024]{1,0:T(8,128)(2,1)S(1)}, u32[]{:S(2)}, u32[]{:S(2)}) collective-permute-start(bf16[128,1024]{1,0:T(8,128)(2,1)S(1)} %get-tuple-element.22), channel_id=1, source_target_pairs={{0,128},{128,256},{256,384},{384,0},{1,129},{129,257},{257,385},{3... | collective-permute-start | bytes 786440 | tf_op jit(solution)/shard_map/ppermute | solution.py:373
